TPU v7x, 32 devices: a whole 2x2x4 slice. The times are simulated.
32 devices in a mesh: groups: 2 (over x), rows: 16 (over z, y, core).
Axes of the slice: x: 2, y: 2, z: 4, core: 2. Of those that a mesh axis runs over, the one named last changes fastest.
Arguments:
- pixels: bfloat16 [128, 16, 512], P(('groups', 'rows')), parts along dimension 0, may hold values from -6 to 6
- weight_first: bfloat16 [3, 3, 512, 512], replicated, may hold values from -0.09375 to 0.09375
- weight_second: bfloat16 [3, 3, 512, 512], replicated, may hold values from -0.09375 to 0.09375
- weight_mix: bfloat16 [3, 3, 2048, 2048], P(None, None, None, 'rows'), may hold values from -0.046875 to 0.046875
- weight_out: bfloat16 [3, 3, 2048, 2048], P(None, None, 'rows'), may hold values from -0.046875 to 0.046875
Outputs:
- latent_out: bfloat16 [32, 4, 2048], P(('groups', 'rows')), parts along dimension 0
There are 2 independent parts, one for each index of `groups`. A program takes and returns all parts, laid end to end along the dimension named above; an argument that names none is the same for every part. Nothing has to cross between parts.
All inputs are finite; a program needn't handle non-finite values.
Results may differ from a plain program's by a relative error of at most 0.014.
Values may be sent and summed in bfloat16 or wider, within the bound.
No kernel may reach another device: no remote copies, remote signals or barrier semaphores. Data moves between devices by JAX's collectives and lax.ppermute only.
A program may use at most 64 MiB of HBM per device.

v0:
```python
import functools

import jax
import jax.numpy as jnp
from jax import lax
from jax.experimental import pallas as pl
from jax.experimental.pallas import tpu as pltpu
from jax.sharding import PartitionSpec as P


F32 = jnp.float32
BF16 = jnp.bfloat16
LOW = 4
LOW_ORDER = (0, 2, 1, 3)
LANES = 128
VMEM = pl.BlockSpec(memory_space=pltpu.VMEM)
COVER = 2 * 10**10


def silu(value):
    return value / (1.0 + jnp.exp(-value))


def flag_of(flags_ref, index):
    return flags_ref[index, :1, :1] != 0


def pick(flag, one, other):
    return jnp.where(flag, one.astype(F32), other.astype(F32))


def place_kernel(bits, last, me_ref, flags_ref):
    me = me_ref[...]
    for bit in range(bits):
        flags_ref[bit] = (me >> bit) & 1
    flags_ref[bits] = (me == 0).astype(jnp.int32)
    flags_ref[bits + 1] = (me == last).astype(jnp.int32)


def placed(me, peers):
    bits = max(1, (peers - 1).bit_length())
    return pl.pallas_call(
        functools.partial(place_kernel, bits, peers - 1),
        out_shape=jax.ShapeDtypeStruct((bits + 2, 8, LANES), jnp.int32),
        in_specs=[VMEM],
        out_specs=VMEM,
        compiler_params=pltpu.CompilerParams(vmem_limit_bytes=2 << 20),
        cost_estimate=pl.CostEstimate(flops=COVER, bytes_accessed=0, transcendentals=0),
        name="place",
    )(jnp.broadcast_to(me, (8, LANES)))


def shift_cols(value, step, width):
    if step == 0:
        return value
    count = value.shape[0]
    moved = pltpu.roll(value, (-step) % count, 0)
    col = lax.broadcasted_iota(jnp.int32, value.shape, 0) % width
    keep = (col + step >= 0) & (col + step < width)
    return jnp.where(keep, moved, 0.0)


def conv_image(feature, weight_ref, width):
    out_rows = feature.shape[0] - 2 * width
    total = None
    for col_tap in (1, 0, 2):
        term = None
        for row_tap in range(3):
            part = jnp.dot(
                feature[row_tap * width : row_tap * width + out_rows],
                weight_ref[row_tap, col_tap],
                preferred_element_type=F32,
            )
            term = part if term is None else term + part
        term = shift_cols(term, col_tap - 1, width)
        total = term if total is None else total + term
    return total


def image_kernel(flags_ref, inner_ref, outer_ref, pixels_ref, first_ref, second_ref, latent_ref, wide_ref, packed_ref):
    rows, width, chans = pixels_ref.shape
    flat = lambda ref: ref[...].reshape(ref.shape[0] * width, chans)
    pixels = flat(pixels_ref)
    odd, bits = flag_of(flags_ref, 0), flags_ref.shape[0] - 2
    inner, outer = flat(inner_ref), flat(outer_ref)
    edge = 2 * width
    before = pick(odd, inner[-edge:], outer[-edge:]).astype(BF16)
    after = pick(odd, outer[:edge], inner[:edge]).astype(BF16)
    extended = jnp.concatenate([before, pixels, after], axis=0)
    activated = silu(conv_image(extended, first_ref, width)).astype(BF16).astype(F32)
    row = lax.broadcasted_iota(jnp.int32, activated.shape, 0) // width
    inside = (row >= flags_ref[bits, :1, :1]) & (row < rows + 2 - flags_ref[bits + 1, :1, :1])
    activated = jnp.where(inside, activated, 0.0).astype(BF16)
    block = pixels.astype(F32) + conv_image(activated, second_ref, width)
    block = block.astype(BF16).astype(F32)
    count = rows * width
    half = ((block + pltpu.roll(block, count - 1, 0)) * 0.5).astype(BF16).astype(F32)
    quarter = ((half + pltpu.roll(half, count - 2, 0)) * 0.5).astype(BF16).astype(F32)
    chunks = chans // LANES
    cols = width // 4
    for chunk in range(chunks):
        wide_ref[chunk] = quarter[:, chunk * LANES : (chunk + 1) * LANES]
    source = lax.broadcasted_iota(jnp.int32, (4 * LANES, 4 * LANES), 0)
    target = lax.broadcasted_iota(jnp.int32, (4 * LANES, 4 * LANES), 1)
    r = source // LANES
    place = (target == 4 * (source % LANES) + 2 * (r % 2) + r // 2).astype(F32).astype(BF16)
    for out_row in range(rows // 4):
        for chunk in range(chunks):
            for sub in range(4):
                start = (4 * out_row + sub) * width
                packed_ref[chunk * cols : (chunk + 1) * cols, sub * LANES : (sub + 1) * LANES] = wide_ref[
                    chunk, pl.ds(start, cols, stride=4), :
                ]
        spread = jnp.dot(packed_ref[...].astype(BF16), place, preferred_element_type=F32)
        for chunk in range(chunks):
            latent_ref[out_row, :, chunk * 4 * LANES : (chunk + 1) * 4 * LANES] = spread[
                chunk * cols : (chunk + 1) * cols
            ].astype(BF16)


def image_stage(flags, inner, outer, pixels, weight_first, weight_second):
    rows, width, chans = pixels.shape
    flops = 2 * 9 * width * chans * chans * (2 * rows + 2)
    moved = 2 * (weight_first.size + weight_second.size + 3 * pixels.size)
    return pl.pallas_call(
        image_kernel,
        out_shape=jax.ShapeDtypeStruct((rows // 4, width // 4, 4 * chans), BF16),
        in_specs=[VMEM] * 6,
        out_specs=VMEM,
        scratch_shapes=[
            pltpu.VMEM((chans // LANES, rows * width, LANES), F32),
            pltpu.VMEM((chans // LANES * (width // 4), 4 * LANES), F32),
        ],
        compiler_params=pltpu.CompilerParams(vmem_limit_bytes=20 << 20),
        cost_estimate=pl.CostEstimate(flops=flops, bytes_accessed=moved, transcendentals=rows * width * chans),
        name="image_stage",
    )(flags, inner, outer, pixels, weight_first, weight_second)


def shift_rows(value, step, block, cols):
    if step == 0:
        return value
    pieces = [value[LOW_ORDER[u] * block : (LOW_ORDER[u] + 1) * block] for u in range(LOW)]
    high = lax.broadcasted_iota(jnp.int32, pieces[0].shape, 0) // cols
    if step > 0:
        wrapped = jnp.where(high < block // cols - 1, pltpu.roll(pieces[0], block - cols, 0), 0.0)
        pieces = pieces[1:] + [wrapped]
    else:
        wrapped = jnp.where(high > 0, pltpu.roll(pieces[-1], cols, 0), 0.0)
        pieces = [wrapped] + pieces[:-1]
    return jnp.concatenate([pieces[u] for u in LOW_ORDER], axis=0)


def halve(total, flags, inner, keep_ref, *send_refs):
    width = len(send_refs) + 1
    for run in range(total.shape[0] // (width * inner)):
        parts = [total[(width * run + k) * inner : (width * run + k + 1) * inner] for k in range(width)]
        for bit, flag in enumerate(flags):
            parts = [jnp.where(flag, parts[k ^ (1 << bit)], parts[k]) for k in range(width)]
        keep_ref[run * inner : (run + 1) * inner] = parts[0]
        for part, send_ref in zip(parts[1:], send_refs):
            send_ref[run * inner : (run + 1) * inner] = part.astype(send_ref.dtype)


def latent_kernel(cols, flags_ref, gathered_ref, mix_ref, out_ref, keep_ref, send_ref):
    feature = gathered_ref[...]
    block = feature.shape[0] // LOW
    hidden_count = mix_ref.shape[3]
    taps = [(a, b) for a in range(3) for b in range(3)]
    terms = {}
    for start in range(0, 9, 2):
        pair = taps[start : start + 2]
        weight = jnp.concatenate([mix_ref[a, b] for a, b in pair], axis=1)
        both = jnp.dot(feature, weight, preferred_element_type=F32)
        for slot, tap in enumerate(pair):
            terms[tap] = both[:, slot * hidden_count : (slot + 1) * hidden_count]
    summed = None
    for a in range(3):
        line = terms[a, 1] + shift_cols(terms[a, 0], -1, cols) + shift_cols(terms[a, 2], 1, cols)
        line = shift_rows(line, a - 1, block, cols)
        summed = line if summed is None else summed + line
    hidden = silu(summed).astype(BF16).astype(F32)
    moved = []
    for a in range(3):
        line = shift_rows(hidden, a - 1, block, cols)
        for b in range(3):
            moved.append(shift_cols(line, b - 1, cols).astype(BF16))
    stacked = jnp.concatenate(moved, axis=1)
    weight = out_ref[...].reshape(9 * hidden_count, out_ref.shape[3])
    total = jnp.dot(stacked, weight, preferred_element_type=F32)
    halve(total, [flag_of(flags_ref, 0)], feature.shape[0] // 2, keep_ref, send_ref)


def latent_stage(flags, gathered, weight_mix, weight_out, cols):
    count, chans = gathered.shape
    flops = 2 * count * (weight_mix.size + weight_out.size)
    moved = 2 * (weight_mix.size + weight_out.size) + 6 * gathered.size
    return pl.pallas_call(
        functools.partial(latent_kernel, cols),
        out_shape=[jax.ShapeDtypeStruct((count // 2, chans), kind) for kind in (F32, BF16)],
        in_specs=[VMEM] * 4,
        out_specs=[VMEM] * 2,
        compiler_params=pltpu.CompilerParams(vmem_limit_bytes=20 << 20),
        cost_estimate=pl.CostEstimate(flops=flops, bytes_accessed=moved, transcendentals=count * weight_mix.shape[3]),
        name="latent_stage",
    )(flags, gathered, weight_mix, weight_out)


def swap(value, peers, bit):
    return lax.ppermute(value, "rows", [(i, i ^ bit) for i in range(peers)])


def halo(value, peers):
    pairs = [(i, i + 1) for i in range(0, peers - 1, 2)], [(i, i + 1) for i in range(1, peers - 1, 2)]
    both = [one + [(j, i) for i, j in one] for one in pairs]
    outer = lax.ppermute(value, "rows", both[1])
    inner = lax.ppermute(value, "rows", both[0])
    return inner, outer


def merge_kernel(index, inner, flags_ref, *refs):
    *blocks, both_ref = refs
    width = len(blocks)
    flags = [flag_of(flags_ref, index + bit) for bit in range((width - 1).bit_length())]
    values = [ref[...].astype(F32) for ref in blocks]
    for block in range(values[0].shape[0] // inner):
        parts = [value[block * inner : (block + 1) * inner] for value in values]
        for bit, flag in enumerate(flags):
            parts = [jnp.where(flag, parts[k ^ (1 << bit)], parts[k]) for k in range(width)]
        for k, part in enumerate(parts):
            start = (width * block + k) * inner
            both_ref[start : start + inner] = part.astype(both_ref.dtype)


def merged(flags, blocks, index, inner, cover=0):
    rows, chans = blocks[0].shape
    return pl.pallas_call(
        functools.partial(merge_kernel, index, inner),
        out_shape=jax.ShapeDtypeStruct((len(blocks) * rows, chans), blocks[0].dtype),
        in_specs=[VMEM] * (1 + len(blocks)),
        out_specs=VMEM,
        compiler_params=pltpu.CompilerParams(vmem_limit_bytes=2 << 20),
        cost_estimate=pl.CostEstimate(flops=cover, bytes_accessed=8 * blocks[0].size, transcendentals=0),
        name="merge",
    )(flags, *blocks)


def exchanged(values, peers, bit):
    got = []
    for k, value in enumerate(values, 1):
        got.append(swap(value, peers, k * bit))
    return got


def gather_rows(latent, flags, peers, cols):
    held = latent
    bit = peers // 2
    while bit >= 4 * LOW:
        held = merged(flags, [held, swap(held, peers, bit)], bit.bit_length() - 1, cols)
        bit //= 2
    far = bit // LOW * 2 - 1
    held = merged(flags, [held, *exchanged([held] * far, peers, LOW)], LOW.bit_length() - 1, cols, COVER)
    bit = LOW // 2
    while bit:
        held = merged(flags, [held, swap(held, peers, bit)], bit.bit_length() - 1, held.shape[0])
        bit //= 2
    return held


def halve_kernel(index, inner, flags_ref, held_ref, got_ref, keep_ref, *send_refs):
    flags = [flag_of(flags_ref, index + bit) for bit in range(len(send_refs).bit_length())]
    halve(held_ref[...] + got_ref[...].astype(F32), flags, inner, keep_ref, *send_refs)


def halved(flags, held, got, index, inner, width=2):
    shape = (held.shape[0] // width, held.shape[1])
    keep, *sends = pl.pallas_call(
        functools.partial(halve_kernel, index, inner),
        out_shape=[jax.ShapeDtypeStruct(shape, kind) for kind in [F32] + [BF16] * (width - 1)],
        in_specs=[VMEM] * 3,
        out_specs=[VMEM] * width,
        compiler_params=pltpu.CompilerParams(vmem_limit_bytes=2 << 20),
        cost_estimate=pl.CostEstimate(flops=held.size, bytes_accessed=6 * held.size, transcendentals=0),
        name="halve",
    )(flags, held, got)
    return keep, sends


def scatter_sum(keep, send, flags, peers, cols):
    bit, sends = 1, [send]
    while 2 * bit < LOW:
        got = swap(sends[0], peers, bit)
        bit *= 2
        keep, sends = halved(flags, keep, got, bit.bit_length() - 1, keep.shape[0] // 2)
    got = swap(sends[0], peers, bit)
    high = peers // LOW
    while high > 4:
        high //= 2
        keep, sends = halved(flags, keep, got, (LOW * high).bit_length() - 1, high * cols)
        got = swap(sends[0], peers, LOW * high)
    keep, sends = halved(flags, keep, got, LOW.bit_length() - 1, cols, high)
    for got in exchanged(sends, peers, LOW):
        keep = keep + got.astype(F32)
    return keep


def plain_latent(latent, weight_mix, weight_out):
    whole = lax.all_gather(latent, "rows", axis=0, tiled=True)

    def conv(value, weight):
        rows, cols = value.shape[:2]
        padded = jnp.pad(value, ((1, 1), (1, 1), (0, 0)))
        summed = 0.0
        for a in range(3):
            for b in range(3):
                summed = summed + jnp.dot(
                    padded[a : a + rows, b : b + cols], weight[a, b], preferred_element_type=F32
                )
        return summed

    hidden = jax.nn.silu(conv(whole, weight_mix)).astype(BF16)
    mixed = lax.psum_scatter(conv(hidden, weight_out), "rows", scatter_dimension=0, tiled=True)
    return (latent.astype(F32) + mixed).astype(BF16)


def compute(pixels, weight_first, weight_second, weight_mix, weight_out):
    peers = lax.axis_size("rows")
    me = lax.axis_index("rows")
    flags = placed(me, peers)
    inner, outer = halo(pixels, peers)
    latent = image_stage(flags, inner, outer, pixels, weight_first, weight_second)
    power = peers >= 2 * LOW and peers & (peers - 1) == 0
    if not power or latent.shape[0] != 1 or weight_mix.shape[3] % LANES:
        return plain_latent(latent, weight_mix, weight_out)
    cols = latent.shape[1]
    gathered = gather_rows(latent[0], flags, peers, cols)
    keep, send = latent_stage(flags, gathered, weight_mix, weight_out, cols)
    mixed = scatter_sum(keep, send, flags, peers, cols)
    return (latent.astype(F32) + mixed[None]).astype(BF16)


def solution(mesh):
    return jax.shard_map(
        compute,
        mesh=mesh,
        in_specs=(
            P(("groups", "rows"), None, None),
            P(),
            P(),
            P(None, None, None, "rows"),
            P(None, None, "rows", None),
        ),
        out_specs=P(("groups", "rows"), None, None),
        check_vma=False,
    )
```

profile of v0, /device:TPU:0, one launch (start us, length us, event | category | flops | bytes accessed | tf_op | source)
XLA Modules:
  0.0 41.4 jit_solution(18391946856073562396)
XLA Ops:
  0.0 0.5 %collective-permute-start = (bf16[4,16,512]{2,1,0:T(8,128)(2,1)}, bf16[4,16,512]{2,1,0:T(8,128)(2,1)S(1)}, u32[]{:S(2)}, u32[]{:S(2)}) collective-permute-start(bf16[4,16,512]{2,1,0:T(8,128)(2,1)} %pixels_ref.1), channel_id=1, source_target_pairs={{0,1},{2,3},{4,5},{6,7},{8,9},{10,11},{12,13},{14,15},{1,0},{3,2},... | collective-permute-start | bytes 196616 | tf_op jit(solution)/shard_map/ppermute | solution.py:217
  0.5 0.7 %collective-permute-start.1 = (bf16[4,16,512]{2,1,0:T(8,128)(2,1)}, bf16[4,16,512]{2,1,0:T(8,128)(2,1)S(1)}, u32[]{:S(2)}, u32[]{:S(2)}) collective-permute-start(bf16[4,16,512]{2,1,0:T(8,128)(2,1)} %pixels_ref.1), channel_id=1, source_target_pairs={{1,2},{3,4},{5,6},{7,8},{9,10},{11,12},{13,14},{2,1},{4,3},{6,5},{... | collective-permute-start | bytes 196616 | tf_op jit(solution)/shard_map/ppermute | solution.py:216
  1.2 0.4 collective-permute-done.inner_ref
  1.6 1.9 %copy-done = bf16[3,3,512,512]{3,2,1,0:T(8,128)(2,1)S(1)} copy-done((bf16[3,3,512,512]{3,2,1,0:T(8,128)(2,1)S(1)}, bf16[3,3,512,512]{3,2,1,0:T(8,128)(2,1)}, u32[]{:S(2)}) %copy-start) | copy-done | bytes 4718616
  3.5 1.4 %copy-done.1 = bf16[3,3,512,512]{3,2,1,0:T(8,128)(2,1)S(1)} copy-done((bf16[3,3,512,512]{3,2,1,0:T(8,128)(2,1)S(1)}, bf16[3,3,512,512]{3,2,1,0:T(8,128)(2,1)}, u32[]{:S(2)}) %copy-start.1) | copy-done | bytes 4718616
  5.0 2.2 %image_stage.1 = bf16[1,4,2048]{2,1,0:T(4,128)(2,1)S(1)} custom-call(s32[6,8,128]{2,1,0:T(8,128)S(1)} %place.1.flags_ref, bf16[4,16,512]{2,1,0:T(8,128)(2,1)S(1)} %collective-permute-done.inner_ref, bf16[4,16,512]{2,1,0:T(8,128)(2,1)S(1)} %collective-permute-done.1.outer_ref, bf16[4,16,512]{2,1,0:T(8,128)(2,1)S(1)} %copy-done.2, ...), custom_call_target="tpu_custom_call" | custom-call | flops 754974720 | bytes 9633792 | tf_op jit(solution)/shard_map/image_stage/pallas_call | solution.py:125
  7.2 7.4 %collective-permute-start.4 = (bf16[4,2048]{1,0:T(4,128)(2,1)S(1)}, bf16[4,2048]{1,0:T(4,128)(2,1)S(1)}, u32[]{:S(2)}, u32[]{:S(2)}) collective-permute-start(bf16[4,2048]{1,0:T(4,128)(2,1)S(1)} %bitcast.9), channel_id=1, source_target_pairs={{0,12},{1,13},{2,14},{3,15},{4,8},{5,9},{6,10},{7,11},{8,4},{9,5},... | collective-permute-start | bytes 49160 | tf_op jit(solution)/shard_map/ppermute | solution.py:210
  14.6 0.6 %collective-permute-start.2 = (bf16[4,2048]{1,0:T(4,128)(2,1)S(1)}, bf16[4,2048]{1,0:T(4,128)(2,1)S(1)}, u32[]{:S(2)}, u32[]{:S(2)}) collective-permute-start(bf16[4,2048]{1,0:T(4,128)(2,1)S(1)} %bitcast.11), channel_id=1, source_target_pairs={{0,4},{1,5},{2,6},{3,7},{4,0},{5,1},{6,2},{7,3},{8,12},{9,13},{10,... | collective-permute-start | bytes 49160 | tf_op jit(solution)/shard_map/ppermute | solution.py:210
  15.2 1.1 %collective-permute-done.4.refs_3_ = bf16[4,2048]{1,0:T(4,128)(2,1)S(1)} collective-permute-done((bf16[4,2048]{1,0:T(4,128)(2,1)S(1)}, bf16[4,2048]{1,0:T(4,128)(2,1)S(1)}, u32[]{:S(2)}, u32[]{:S(2)}) %collective-permute-start.4) | collective-permute-done | bytes 16416 | tf_op jit(solution)/shard_map/ppermute | solution.py:210
  16.3 2.9 %collective-permute-done.3.refs_2_ = bf16[4,2048]{1,0:T(4,128)(2,1)S(1)} collective-permute-done((bf16[4,2048]{1,0:T(4,128)(2,1)S(1)}, bf16[4,2048]{1,0:T(4,128)(2,1)S(1)}, u32[]{:S(2)}, u32[]{:S(2)}) %collective-permute-start.3) | collective-permute-done | bytes 16416 | tf_op jit(solution)/shard_map/ppermute | solution.py:210
  19.3 0.7 %collective-permute-start.5 = (bf16[16,2048]{1,0:T(8,128)(2,1)S(1)}, bf16[16,2048]{1,0:T(8,128)(2,1)S(1)}, u32[]{:S(2)}, u32[]{:S(2)}) collective-permute-start(bf16[16,2048]{1,0:T(8,128)(2,1)S(1)} %merge.3.refs_0_), channel_id=1, source_target_pairs={{0,2},{1,3},{2,0},{3,1},{4,6},{5,7},{6,4},{7,5},{8,10},{9,11},{10,... | collective-permute-start | bytes 196616 | tf_op jit(solution)/shard_map/ppermute | solution.py:210
  20.0 3.6 %collective-permute-done.5.refs_1_ = bf16[16,2048]{1,0:T(8,128)(2,1)S(1)} collective-permute-done((bf16[16,2048]{1,0:T(8,128)(2,1)S(1)}, bf16[16,2048]{1,0:T(8,128)(2,1)S(1)}, u32[]{:S(2)}, u32[]{:S(2)}) %collective-permute-start.5) | collective-permute-done | bytes 65568 | tf_op jit(solution)/shard_map/ppermute | solution.py:210
  23.8 1.3 %collective-permute-done.6.refs_1_ = bf16[32,2048]{1,0:T(8,128)(2,1)S(1)} collective-permute-done((bf16[32,2048]{1,0:T(8,128)(2,1)S(1)}, bf16[32,2048]{1,0:T(8,128)(2,1)S(1)}, u32[]{:S(2)}, u32[]{:S(2)}) %collective-permute-start.6) | collective-permute-done | bytes 131104 | tf_op jit(solution)/shard_map/ppermute | solution.py:210
  25.1 0.1 merge.5.gathered_ref
  25.3 1.9 %latent_stage.1 = (f32[32,2048]{1,0:T(8,128)S(1)}, bf16[32,2048]{1,0:T(8,128)(2,1)S(1)}) custom-call(s32[6,8,128]{2,1,0:T(8,128)S(1)} %place.1.flags_ref, bf16[64,2048]{1,0:T(8,128)(2,1)S(1)} %merge.5.gathered_ref, bf16[3,3,2048,128]{3,2,1,0:T(8,128)(2,1)S(1)} %bitcast.6, bf16[3,3,128,2048]{3,2,1,0:T(8,128)(2,1)S(1)} %bitcast.8), custom_call_target="tpu_custom_call" | custom-call | flops 603979776 | bytes 10223616 | tf_op jit(solution)/shard_map/latent_stage/pallas_call | solution.py:198
  27.2 0.2 collective-permute-start.7
  27.4 1.2 %collective-permute-done.7.got_ref = bf16[32,2048]{1,0:T(8,128)(2,1)S(1)} collective-permute-done((bf16[32,2048]{1,0:T(8,128)(2,1)S(1)}, bf16[32,2048]{1,0:T(8,128)(2,1)S(1)}, u32[]{:S(2)}, u32[]{:S(2)}) %collective-permute-start.7) | collective-permute-done | bytes 131104 | tf_op jit(solution)/shard_map/ppermute | solution.py:210
  28.6 0.7 %collective-permute-start.8 = (bf16[16,2048]{1,0:T(8,128)(2,1)S(1)}, bf16[16,2048]{1,0:T(8,128)(2,1)S(1)}, u32[]{:S(2)}, u32[]{:S(2)}) collective-permute-start(bf16[16,2048]{1,0:T(8,128)(2,1)S(1)} %get-tuple-element.16), channel_id=1, source_target_pairs={{0,2},{1,3},{2,0},{3,1},{4,6},{5,7},{6,4},{7,5},{8,10},{9,11},{10,... | collective-permute-start | bytes 196616 | tf_op jit(solution)/shard_map/ppermute | solution.py:210
  29.3 3.6 %collective-permute-done.8.got_ref = bf16[16,2048]{1,0:T(8,128)(2,1)S(1)} collective-permute-done((bf16[16,2048]{1,0:T(8,128)(2,1)S(1)}, bf16[16,2048]{1,0:T(8,128)(2,1)S(1)}, u32[]{:S(2)}, u32[]{:S(2)}) %collective-permute-start.8) | collective-permute-done | bytes 65568 | tf_op jit(solution)/shard_map/ppermute | solution.py:210
  33.1 2.1 %collective-permute-start.10 = (bf16[4,2048]{1,0:T(4,128)(2,1)S(1)}, bf16[4,2048]{1,0:T(4,128)(2,1)S(1)}, u32[]{:S(2)}, u32[]{:S(2)}) collective-permute-start(bf16[4,2048]{1,0:T(4,128)(2,1)S(1)} %get-tuple-element.19), channel_id=1, source_target_pairs={{0,8},{1,9},{2,10},{3,11},{4,12},{5,13},{6,14},{7,15},{8,0},{9,1},... | collective-permute-start | bytes 49160 | tf_op jit(solution)/shard_map/ppermute | solution.py:210
  35.2 2.3 %collective-permute-start.11 = (bf16[4,2048]{1,0:T(4,128)(2,1)S(1)}, bf16[4,2048]{1,0:T(4,128)(2,1)S(1)}, u32[]{:S(2)}, u32[]{:S(2)}) collective-permute-start(bf16[4,2048]{1,0:T(4,128)(2,1)S(1)} %get-tuple-element.20), channel_id=1, source_target_pairs={{0,12},{1,13},{2,14},{3,15},{4,8},{5,9},{6,10},{7,11},{8,4},{9,5},... | collective-permute-start | bytes 49160 | tf_op jit(solution)/shard_map/ppermute | solution.py:210
  37.5 0.5 %collective-permute-done.10 = bf16[4,2048]{1,0:T(4,128)(2,1)S(1)} collective-permute-done((bf16[4,2048]{1,0:T(4,128)(2,1)S(1)}, bf16[4,2048]{1,0:T(4,128)(2,1)S(1)}, u32[]{:S(2)}, u32[]{:S(2)}) %collective-permute-start.10) | collective-permute-done | bytes 16416 | tf_op jit(solution)/shard_map/ppermute | solution.py:210
  38.0 2.8 %collective-permute-done.11 = bf16[4,2048]{1,0:T(4,128)(2,1)S(1)} collective-permute-done((bf16[4,2048]{1,0:T(4,128)(2,1)S(1)}, bf16[4,2048]{1,0:T(4,128)(2,1)S(1)}, u32[]{:S(2)}, u32[]{:S(2)}) %collective-permute-start.11) | collective-permute-done | bytes 16416 | tf_op jit(solution)/shard_map/ppermute | solution.py:210
  40.7 0.6 %fusion = bf16[1,4,2048]{2,1,0:T(4,128)(2,1)} fusion(bf16[4,2048]{1,0:T(4,128)(2,1)S(1)} %collective-permute-done.11, bf16[4,2048]{1,0:T(4,128)(2,1)S(1)} %collective-permute-done.10, f32[4,2048]{1,0:T(4,128)S(1)} %get-tuple-element.17, bf16[4,2048]{1,0:T(4,128)(2,1)S(1)} %collective-permute-done.9, bf16[1,4,2048]{2,1,0:T(4,128)(2,1)S(1)} %image_stage.1), kind=kLoop, calls=%fused_computation.1 | loop fusion | flops 73728 | bytes 114688 | tf_op jit(solution)/shard_map/convert_element_type | solution.py:339
  (26 shorter events, 0.4 us)
Async XLA Ops:
  0.0 1.6 %collective-permute-start = (bf16[4,16,512]{2,1,0:T(8,128)(2,1)}, bf16[4,16,512]{2,1,0:T(8,128)(2,1)S(1)}, u32[]{:S(2)}, u32[]{:S(2)}) collective-permute-start(bf16[4,16,512]{2,1,0:T(8,128)(2,1)} %pixels_ref.1), channel_id=1, source_target_pairs={{0,1},{2,3},{4,5},{6,7},{8,9},{10,11},{12,13},{14,15},{1,0},{3,2},... | collective-permute-start | bytes 196616 | tf_op jit(solution)/shard_map/ppermute | solution.py:217
  0.5 1.1 %collective-permute-start.1 = (bf16[4,16,512]{2,1,0:T(8,128)(2,1)}, bf16[4,16,512]{2,1,0:T(8,128)(2,1)S(1)}, u32[]{:S(2)}, u32[]{:S(2)}) collective-permute-start(bf16[4,16,512]{2,1,0:T(8,128)(2,1)} %pixels_ref.1), channel_id=1, source_target_pairs={{1,2},{3,4},{5,6},{7,8},{9,10},{11,12},{13,14},{2,1},{4,3},{6,5},{... | collective-permute-start | bytes 196616 | tf_op jit(solution)/shard_map/ppermute | solution.py:216
  1.2 2.3 %copy-start = (bf16[3,3,512,512]{3,2,1,0:T(8,128)(2,1)S(1)}, bf16[3,3,512,512]{3,2,1,0:T(8,128)(2,1)}, u32[]{:S(2)}) copy-start(bf16[3,3,512,512]{3,2,1,0:T(8,128)(2,1)} %first_ref.1) | copy-start | bytes 14155780
  1.2 3.8 %copy-start.1 = (bf16[3,3,512,512]{3,2,1,0:T(8,128)(2,1)S(1)}, bf16[3,3,512,512]{3,2,1,0:T(8,128)(2,1)}, u32[]{:S(2)}) copy-start(bf16[3,3,512,512]{3,2,1,0:T(8,128)(2,1)} %second_ref.1) | copy-start | bytes 14155780
  1.2 3.8 %copy-start.2 = (bf16[4,16,512]{2,1,0:T(8,128)(2,1)S(1)}, bf16[4,16,512]{2,1,0:T(8,128)(2,1)}, u32[]{:S(2)}) copy-start(bf16[4,16,512]{2,1,0:T(8,128)(2,1)} %pixels_ref.1) | copy-start | bytes 196612
  7.1 18.1 %slice-start = ((s8[4718592]{0:T(1024)(128)(4,1)}), s8[4194304]{0:T(1024)(128)(4,1)S(1)}, s32[]{:S(2)}) async-start(s8[4718592]{0:T(1024)(128)(4,1)} %bitcast.5), calls=%async_computation | async-start | bytes 8388608
  7.1 18.1 %slice-start.2 = ((s8[4718592]{0:T(1024)(128)(4,1)}), s8[4194304]{0:T(1024)(128)(4,1)S(1)}, s32[]{:S(2)}) async-start(s8[4718592]{0:T(1024)(128)(4,1)} %bitcast.7), calls=%async_computation.2 | async-start | bytes 8388608
  7.1 18.1 %slice-start.1 = ((s8[4718592]{0:T(1024)(128)(4,1)}), s8[524288]{0:T(1024)(128)(4,1)S(1)}, s32[]{:S(2)}) async-start(s8[4718592]{0:T(1024)(128)(4,1)} %bitcast.5), calls=%async_computation.1 | async-start | bytes 1048576
  7.2 18.1 %slice-start.3 = ((s8[4718592]{0:T(1024)(128)(4,1)}), s8[524288]{0:T(1024)(128)(4,1)S(1)}, s32[]{:S(2)}) async-start(s8[4718592]{0:T(1024)(128)(4,1)} %bitcast.7), calls=%async_computation.3 | async-start | bytes 1048576
  7.2 9.1 %collective-permute-start.4 = (bf16[4,2048]{1,0:T(4,128)(2,1)S(1)}, bf16[4,2048]{1,0:T(4,128)(2,1)S(1)}, u32[]{:S(2)}, u32[]{:S(2)}) collective-permute-start(bf16[4,2048]{1,0:T(4,128)(2,1)S(1)} %bitcast.9), channel_id=1, source_target_pairs={{0,12},{1,13},{2,14},{3,15},{4,8},{5,9},{6,10},{7,11},{8,4},{9,5},... | collective-permute-start | bytes 49160 | tf_op jit(solution)/shard_map/ppermute | solution.py:210
  14.6 4.6 %collective-permute-start.3 = (bf16[4,2048]{1,0:T(4,128)(2,1)S(1)}, bf16[4,2048]{1,0:T(4,128)(2,1)S(1)}, u32[]{:S(2)}, u32[]{:S(2)}) collective-permute-start(bf16[4,2048]{1,0:T(4,128)(2,1)S(1)} %bitcast.10), channel_id=1, source_target_pairs={{0,8},{1,9},{2,10},{3,11},{4,12},{5,13},{6,14},{7,15},{8,0},{9,1},... | collective-permute-start | bytes 49160 | tf_op jit(solution)/shard_map/ppermute | solution.py:210
  14.6 4.6 %collective-permute-start.2 = (bf16[4,2048]{1,0:T(4,128)(2,1)S(1)}, bf16[4,2048]{1,0:T(4,128)(2,1)S(1)}, u32[]{:S(2)}, u32[]{:S(2)}) collective-permute-start(bf16[4,2048]{1,0:T(4,128)(2,1)S(1)} %bitcast.11), channel_id=1, source_target_pairs={{0,4},{1,5},{2,6},{3,7},{4,0},{5,1},{6,2},{7,3},{8,12},{9,13},{10,... | collective-permute-start | bytes 49160 | tf_op jit(solution)/shard_map/ppermute | solution.py:210
  19.3 4.3 %collective-permute-start.5 = (bf16[16,2048]{1,0:T(8,128)(2,1)S(1)}, bf16[16,2048]{1,0:T(8,128)(2,1)S(1)}, u32[]{:S(2)}, u32[]{:S(2)}) collective-permute-start(bf16[16,2048]{1,0:T(8,128)(2,1)S(1)} %merge.3.refs_0_), channel_id=1, source_target_pairs={{0,2},{1,3},{2,0},{3,1},{4,6},{5,7},{6,4},{7,5},{8,10},{9,11},{10,... | collective-permute-start | bytes 196616 | tf_op jit(solution)/shard_map/ppermute | solution.py:210
  23.7 1.4 %collective-permute-start.6 = (bf16[32,2048]{1,0:T(8,128)(2,1)S(1)}, bf16[32,2048]{1,0:T(8,128)(2,1)S(1)}, u32[]{:S(2)}, u32[]{:S(2)}) collective-permute-start(bf16[32,2048]{1,0:T(8,128)(2,1)S(1)} %merge.4.refs_0_), channel_id=1, source_target_pairs={{0,1},{1,0},{2,3},{3,2},{4,5},{5,4},{6,7},{7,6},{8,9},{9,8},{10,11... | collective-permute-start | bytes 393224 | tf_op jit(solution)/shard_map/ppermute | solution.py:210
  27.2 1.4 %collective-permute-start.7 = (bf16[32,2048]{1,0:T(8,128)(2,1)S(1)}, bf16[32,2048]{1,0:T(8,128)(2,1)S(1)}, u32[]{:S(2)}, u32[]{:S(2)}) collective-permute-start(bf16[32,2048]{1,0:T(8,128)(2,1)S(1)} %get-tuple-element.14), channel_id=1, source_target_pairs={{0,1},{1,0},{2,3},{3,2},{4,5},{5,4},{6,7},{7,6},{8,9},{9,8},{10,11... | collective-permute-start | bytes 393224 | tf_op jit(solution)/shard_map/ppermute | solution.py:210
  28.6 4.3 %collective-permute-start.8 = (bf16[16,2048]{1,0:T(8,128)(2,1)S(1)}, bf16[16,2048]{1,0:T(8,128)(2,1)S(1)}, u32[]{:S(2)}, u32[]{:S(2)}) collective-permute-start(bf16[16,2048]{1,0:T(8,128)(2,1)S(1)} %get-tuple-element.16), channel_id=1, source_target_pairs={{0,2},{1,3},{2,0},{3,1},{4,6},{5,7},{6,4},{7,5},{8,10},{9,11},{10,... | collective-permute-start | bytes 196616 | tf_op jit(solution)/shard_map/ppermute | solution.py:210
  33.0 4.5 %collective-permute-start.9 = (bf16[4,2048]{1,0:T(4,128)(2,1)S(1)}, bf16[4,2048]{1,0:T(4,128)(2,1)S(1)}, u32[]{:S(2)}, u32[]{:S(2)}) collective-permute-start(bf16[4,2048]{1,0:T(4,128)(2,1)S(1)} %get-tuple-element.18), channel_id=1, source_target_pairs={{0,4},{1,5},{2,6},{3,7},{4,0},{5,1},{6,2},{7,3},{8,12},{9,13},{10,... | collective-permute-start | bytes 49160 | tf_op jit(solution)/shard_map/ppermute | solution.py:210
  33.1 4.9 %collective-permute-start.10 = (bf16[4,2048]{1,0:T(4,128)(2,1)S(1)}, bf16[4,2048]{1,0:T(4,128)(2,1)S(1)}, u32[]{:S(2)}, u32[]{:S(2)}) collective-permute-start(bf16[4,2048]{1,0:T(4,128)(2,1)S(1)} %get-tuple-element.19), channel_id=1, source_target_pairs={{0,8},{1,9},{2,10},{3,11},{4,12},{5,13},{6,14},{7,15},{8,0},{9,1},... | collective-permute-start | bytes 49160 | tf_op jit(solution)/shard_map/ppermute | solution.py:210
  35.2 5.5 %collective-permute-start.11 = (bf16[4,2048]{1,0:T(4,128)(2,1)S(1)}, bf16[4,2048]{1,0:T(4,128)(2,1)S(1)}, u32[]{:S(2)}, u32[]{:S(2)}) collective-permute-start(bf16[4,2048]{1,0:T(4,128)(2,1)S(1)} %get-tuple-element.20), channel_id=1, source_target_pairs={{0,12},{1,13},{2,14},{3,15},{4,8},{5,9},{6,10},{7,11},{8,4},{9,5},... | collective-permute-start | bytes 49160 | tf_op jit(solution)/shard_map/ppermute | solution.py:210
where the time goes:
time: 41.5 us; the launch traced here: 41.4 us
  waiting for transfers between devices  17.5 us (42%)
  starting transfers between devices  15.3 us (37%)
  Pallas kernels  4.41 us (11%)
  local copies, waits for them, and re-layouts  3.37 us (8%)
  other arithmetic  0.63 us (2%)
    ppermute x10, waiting for transfers between devices, swap(): return lax.ppermute(value, 'rows', [(i, i ^ bit) for i in range(peers)])  17.1 us
    ppermute x10, starting transfers between devices, swap(): return lax.ppermute(value, 'rows', [(i, i ^ bit) for i in range(peers)])  14.2 us
    unnamed x14, local copies, waits for them, and re-layouts  3.37 us
    pallas_call x1, Pallas kernels, image_stage(): pl.pallas_call(image_kernel, out_shape=jax.ShapeDtypeStruct((rows // 4, w...  2.18 us
    pallas_call x1, Pallas kernels, latent_stage(): pl.pallas_call(functools.partial(latent_kernel, cols), out_shape=[jax.Sha...  1.87 us
  transfers between devices with their start and end apart: 12, of which 9 were waited for; matrix products, arithmetic and copies ran while one was open for 0% of the time, Pallas kernels for 0%

commit v1 on v0

--- a/solution.py
+++ b/solution.py
@@ -12,6 +12,8 @@
 BF16 = jnp.bfloat16
 LOW = 4
 LOW_ORDER = (0, 2, 1, 3)
+LINE = 4
+NEAR_FLIP, FAR_FLIP, SIDE_FLIP = 0, 1, 1
 LANES = 128
 VMEM = pl.BlockSpec(memory_space=pltpu.VMEM)
 COVER = 2 * 10**10
@@ -27,6 +29,10 @@
 
 def pick(flag, one, other):
     return jnp.where(flag, one.astype(F32), other.astype(F32))
+
+
+def kind_of(core, side, place):
+    return core ^ (SIDE_FLIP * side) ^ (NEAR_FLIP * (place & 1)) ^ (FAR_FLIP * (place >> 1))
 
 
 def place_kernel(bits, last, me_ref, flags_ref):
@@ -35,13 +41,14 @@
         flags_ref[bit] = (me >> bit) & 1
     flags_ref[bits] = (me == 0).astype(jnp.int32)
     flags_ref[bits + 1] = (me == last).astype(jnp.int32)
+    flags_ref[bits + 2] = kind_of(me & 1, (me >> 1) & 1, (me >> 2) & 3)
 
 
 def placed(me, peers):
     bits = max(1, (peers - 1).bit_length())
     return pl.pallas_call(
         functools.partial(place_kernel, bits, peers - 1),
-        out_shape=jax.ShapeDtypeStruct((bits + 2, 8, LANES), jnp.int32),
+        out_shape=jax.ShapeDtypeStruct((bits + 3, 8, LANES), jnp.int32),
         in_specs=[VMEM],
         out_specs=VMEM,
         compiler_params=pltpu.CompilerParams(vmem_limit_bytes=2 << 20),
@@ -81,7 +88,7 @@
     rows, width, chans = pixels_ref.shape
     flat = lambda ref: ref[...].reshape(ref.shape[0] * width, chans)
     pixels = flat(pixels_ref)
-    odd, bits = flag_of(flags_ref, 0), flags_ref.shape[0] - 2
+    odd, bits = flag_of(flags_ref, 0), flags_ref.shape[0] - 3
     inner, outer = flat(inner_ref), flat(outer_ref)
     edge = 2 * width
     before = pick(odd, inner[-edge:], outer[-edge:]).astype(BF16)
@@ -151,6 +158,14 @@
     return jnp.concatenate([pieces[u] for u in LOW_ORDER], axis=0)
 
 
+SPOTS = [(side, place) for side in range(LOW // 2) for place in range(LINE)]
+
+
+def block_of(value, core, side, place, cols):
+    start = ((core * (LOW // 2) + side) * LINE + place) * cols
+    return value[start : start + cols]
+
+
 def halve(total, flags, inner, keep_ref, *send_refs):
     width = len(send_refs) + 1
     for run in range(total.shape[0] // (width * inner)):
@@ -188,7 +203,11 @@
     stacked = jnp.concatenate(moved, axis=1)
     weight = out_ref[...].reshape(9 * hidden_count, out_ref.shape[3])
     total = jnp.dot(stacked, weight, preferred_element_type=F32)
-    halve(total, [flag_of(flags_ref, 0)], feature.shape[0] // 2, keep_ref, send_ref)
+    kind = flag_of(flags_ref, flags_ref.shape[0] - 1)
+    for index, (side, place) in enumerate(SPOTS):
+        first, second = [block_of(total, kind_of(which, side, place), side, place, cols) for which in range(2)]
+        keep_ref[index * cols : (index + 1) * cols] = pick(kind, second, first)
+        send_ref[index * cols : (index + 1) * cols] = pick(kind, first, second).astype(send_ref.dtype)
 
 
 def latent_stage(flags, gathered, weight_mix, weight_out, cols):
@@ -232,6 +251,31 @@
             both_ref[start : start + inner] = part.astype(both_ref.dtype)
 
 
+def unite_kernel(flags_ref, own_ref, got_ref, both_ref):
+    kind = flag_of(flags_ref, flags_ref.shape[0] - 1)
+    own, got = own_ref[...].astype(F32), got_ref[...].astype(F32)
+    kinds = [pick(kind, got, own), pick(kind, own, got)]
+    cols = own.shape[0] // len(SPOTS)
+    for index, (side, place) in enumerate(SPOTS):
+        for core in range(2):
+            start = ((core * (LOW // 2) + side) * LINE + place) * cols
+            block = kinds[kind_of(core, side, place)][index * cols : (index + 1) * cols]
+            both_ref[start : start + cols] = block.astype(both_ref.dtype)
+
+
+def united(flags, own, got):
+    rows, chans = own.shape
+    return pl.pallas_call(
+        unite_kernel,
+        out_shape=jax.ShapeDtypeStruct((2 * rows, chans), own.dtype),
+        in_specs=[VMEM] * 3,
+        out_specs=VMEM,
+        compiler_params=pltpu.CompilerParams(vmem_limit_bytes=2 << 20),
+        cost_estimate=pl.CostEstimate(flops=0, bytes_accessed=8 * own.size, transcendentals=0),
+        name="unite",
+    )(flags, own, got)
+
+
 def merged(flags, blocks, index, inner, cover=0):
     rows, chans = blocks[0].shape
     return pl.pallas_call(
@@ -245,26 +289,17 @@
     )(flags, *blocks)
 
 
-def exchanged(values, peers, bit):
+def exchanged(values, peers):
     got = []
     for k, value in enumerate(values, 1):
-        got.append(swap(value, peers, k * bit))
+        got.append(swap(value, peers, LOW * k + kind_of(0, 0, k)))
     return got
 
 
 def gather_rows(latent, flags, peers, cols):
-    held = latent
-    bit = peers // 2
-    while bit >= 4 * LOW:
-        held = merged(flags, [held, swap(held, peers, bit)], bit.bit_length() - 1, cols)
-        bit //= 2
-    far = bit // LOW * 2 - 1
-    held = merged(flags, [held, *exchanged([held] * far, peers, LOW)], LOW.bit_length() - 1, cols, COVER)
-    bit = LOW // 2
-    while bit:
-        held = merged(flags, [held, swap(held, peers, bit)], bit.bit_length() - 1, held.shape[0])
-        bit //= 2
-    return held
+    held = merged(flags, [latent, *exchanged([latent] * (LINE - 1), peers)], LOW.bit_length() - 1, cols, COVER)
+    held = merged(flags, [held, swap(held, peers, 2 + SIDE_FLIP)], 1, held.shape[0])
+    return united(flags, held, swap(held, peers, 1))
 
 
 def halve_kernel(index, inner, flags_ref, held_ref, got_ref, keep_ref, *send_refs):
@@ -287,19 +322,11 @@
 
 
 def scatter_sum(keep, send, flags, peers, cols):
-    bit, sends = 1, [send]
-    while 2 * bit < LOW:
-        got = swap(sends[0], peers, bit)
-        bit *= 2
-        keep, sends = halved(flags, keep, got, bit.bit_length() - 1, keep.shape[0] // 2)
-    got = swap(sends[0], peers, bit)
-    high = peers // LOW
-    while high > 4:
-        high //= 2
-        keep, sends = halved(flags, keep, got, (LOW * high).bit_length() - 1, high * cols)
-        got = swap(sends[0], peers, LOW * high)
-    keep, sends = halved(flags, keep, got, LOW.bit_length() - 1, cols, high)
-    for got in exchanged(sends, peers, LOW):
+    got = swap(send, peers, 1)
+    keep, sends = halved(flags, keep, got, 1, LINE * cols)
+    got = swap(sends[0], peers, 2 + SIDE_FLIP)
+    keep, sends = halved(flags, keep, got, LOW.bit_length() - 1, cols, LINE)
+    for got in exchanged(sends, peers):
         keep = keep + got.astype(F32)
     return keep
 
@@ -329,8 +356,7 @@
     flags = placed(me, peers)
     inner, outer = halo(pixels, peers)
     latent = image_stage(flags, inner, outer, pixels, weight_first, weight_second)
-    power = peers >= 2 * LOW and peers & (peers - 1) == 0
-    if not power or latent.shape[0] != 1 or weight_mix.shape[3] % LANES:
+    if peers != LINE * LOW or latent.shape[0] != 1 or weight_mix.shape[3] % LANES:
         return plain_latent(latent, weight_mix, weight_out)
     cols = latent.shape[1]
     gathered = gather_rows(latent[0], flags, peers, cols)

time: 41.5 us -> 39.8 us (0.959)
  waiting for transfers between devices: 17.5 us -> 15.7 us
    ppermute x10, waiting for transfers between devices: 17.1 us -> 15.3 us  [swap(): return lax.ppermute(value, 'rows', [(i, i ^ bit) for i in range(peers)])]
where the time goes in v1:
time: 39.8 us; the launch traced here: 39.5 us
  waiting for transfers between devices  15.7 us (39%)
  starting transfers between devices  15.2 us (38%)
  Pallas kernels  4.42 us (11%)
  local copies, waits for them, and re-layouts  3.37 us (8%)
  other arithmetic  0.63 us (2%)
    ppermute x10, waiting for transfers between devices, swap(): return lax.ppermute(value, 'rows', [(i, i ^ bit) for i in range(peers)])  15.3 us
    ppermute x10, starting transfers between devices, swap(): return lax.ppermute(value, 'rows', [(i, i ^ bit) for i in range(peers)])  14 us
    unnamed x14, local copies, waits for them, and re-layouts  3.37 us
    pallas_call x1, Pallas kernels, image_stage(): pl.pallas_call(image_kernel, out_shape=jax.ShapeDtypeStruct((rows // 4, w...  2.19 us
    pallas_call x1, Pallas kernels, latent_stage(): pl.pallas_call(functools.partial(latent_kernel, cols), out_shape=[jax.Sha...  1.86 us
  transfers between devices with their start and end apart: 12, of which 9 were waited for; matrix products, arithmetic and copies ran while one was open for 0% of the time, Pallas kernels for 0%

profile of v1, /device:TPU:0, one launch (start us, length us, event | category | flops | bytes accessed | tf_op | source)
XLA Modules:
  0.0 39.5 jit_solution(17048586565852450856)
XLA Ops:
  0.0 0.5 %collective-permute-start = (bf16[4,16,512]{2,1,0:T(8,128)(2,1)}, bf16[4,16,512]{2,1,0:T(8,128)(2,1)S(1)}, u32[]{:S(2)}, u32[]{:S(2)}) collective-permute-start(bf16[4,16,512]{2,1,0:T(8,128)(2,1)} %pixels_ref.1), channel_id=1, source_target_pairs={{0,1},{2,3},{4,5},{6,7},{8,9},{10,11},{12,13},{14,15},{1,0},{3,2},... | collective-permute-start | bytes 196616 | tf_op jit(solution)/shard_map/ppermute | solution.py:236
  0.5 0.7 %collective-permute-start.1 = (bf16[4,16,512]{2,1,0:T(8,128)(2,1)}, bf16[4,16,512]{2,1,0:T(8,128)(2,1)S(1)}, u32[]{:S(2)}, u32[]{:S(2)}) collective-permute-start(bf16[4,16,512]{2,1,0:T(8,128)(2,1)} %pixels_ref.1), channel_id=1, source_target_pairs={{1,2},{3,4},{5,6},{7,8},{9,10},{11,12},{13,14},{2,1},{4,3},{6,5},{... | collective-permute-start | bytes 196616 | tf_op jit(solution)/shard_map/ppermute | solution.py:235
  1.6 1.9 %copy-done = bf16[3,3,512,512]{3,2,1,0:T(8,128)(2,1)S(1)} copy-done((bf16[3,3,512,512]{3,2,1,0:T(8,128)(2,1)S(1)}, bf16[3,3,512,512]{3,2,1,0:T(8,128)(2,1)}, u32[]{:S(2)}) %copy-start) | copy-done | bytes 4718616
  3.5 1.4 %copy-done.1 = bf16[3,3,512,512]{3,2,1,0:T(8,128)(2,1)S(1)} copy-done((bf16[3,3,512,512]{3,2,1,0:T(8,128)(2,1)S(1)}, bf16[3,3,512,512]{3,2,1,0:T(8,128)(2,1)}, u32[]{:S(2)}) %copy-start.1) | copy-done | bytes 4718616
  5.0 2.2 %image_stage.1 = bf16[1,4,2048]{2,1,0:T(4,128)(2,1)S(1)} custom-call(s32[7,8,128]{2,1,0:T(8,128)S(1)} %place.1.flags_ref, bf16[4,16,512]{2,1,0:T(8,128)(2,1)S(1)} %collective-permute-done.inner_ref, bf16[4,16,512]{2,1,0:T(8,128)(2,1)S(1)} %collective-permute-done.1.outer_ref, bf16[4,16,512]{2,1,0:T(8,128)(2,1)S(1)} %copy-done.2, ...), custom_call_target="tpu_custom_call" | custom-call | flops 754974720 | bytes 9633792 | tf_op jit(solution)/shard_map/image_stage/pallas_call | solution.py:132
  7.2 7.1 %collective-permute-start.4 = (bf16[4,2048]{1,0:T(4,128)(2,1)S(1)}, bf16[4,2048]{1,0:T(4,128)(2,1)S(1)}, u32[]{:S(2)}, u32[]{:S(2)}) collective-permute-start(bf16[4,2048]{1,0:T(4,128)(2,1)S(1)} %bitcast.9), channel_id=1, source_target_pairs={{0,13},{1,12},{2,15},{3,14},{4,9},{5,8},{6,11},{7,10},{8,5},{9,4},... | collective-permute-start | bytes 49160 | tf_op jit(solution)/shard_map/ppermute | solution.py:229
  14.3 0.6 %collective-permute-start.2 = (bf16[4,2048]{1,0:T(4,128)(2,1)S(1)}, bf16[4,2048]{1,0:T(4,128)(2,1)S(1)}, u32[]{:S(2)}, u32[]{:S(2)}) collective-permute-start(bf16[4,2048]{1,0:T(4,128)(2,1)S(1)} %bitcast.11), channel_id=1, source_target_pairs={{0,4},{1,5},{2,6},{3,7},{4,0},{5,1},{6,2},{7,3},{8,12},{9,13},{10,... | collective-permute-start | bytes 49160 | tf_op jit(solution)/shard_map/ppermute | solution.py:229
  15.0 0.8 %collective-permute-done.4.refs_3_ = bf16[4,2048]{1,0:T(4,128)(2,1)S(1)} collective-permute-done((bf16[4,2048]{1,0:T(4,128)(2,1)S(1)}, bf16[4,2048]{1,0:T(4,128)(2,1)S(1)}, u32[]{:S(2)}, u32[]{:S(2)}) %collective-permute-start.4) | collective-permute-done | bytes 16416 | tf_op jit(solution)/shard_map/ppermute | solution.py:229
  15.8 2.6 %collective-permute-done.3.refs_2_ = bf16[4,2048]{1,0:T(4,128)(2,1)S(1)} collective-permute-done((bf16[4,2048]{1,0:T(4,128)(2,1)S(1)}, bf16[4,2048]{1,0:T(4,128)(2,1)S(1)}, u32[]{:S(2)}, u32[]{:S(2)}) %collective-permute-start.3) | collective-permute-done | bytes 16416 | tf_op jit(solution)/shard_map/ppermute | solution.py:229
  18.4 0.7 %collective-permute-start.5 = (bf16[16,2048]{1,0:T(8,128)(2,1)S(1)}, bf16[16,2048]{1,0:T(8,128)(2,1)S(1)}, u32[]{:S(2)}, u32[]{:S(2)}) collective-permute-start(bf16[16,2048]{1,0:T(8,128)(2,1)S(1)} %merge.2.refs_0_), channel_id=1, source_target_pairs={{0,3},{1,2},{2,1},{3,0},{4,7},{5,6},{6,5},{7,4},{8,11},{9,10},{10,... | collective-permute-start | bytes 196616 | tf_op jit(solution)/shard_map/ppermute | solution.py:229
  19.1 3.2 %collective-permute-done.5.refs_1_ = bf16[16,2048]{1,0:T(8,128)(2,1)S(1)} collective-permute-done((bf16[16,2048]{1,0:T(8,128)(2,1)S(1)}, bf16[16,2048]{1,0:T(8,128)(2,1)S(1)}, u32[]{:S(2)}, u32[]{:S(2)}) %collective-permute-start.5) | collective-permute-done | bytes 65568 | tf_op jit(solution)/shard_map/ppermute | solution.py:229
  22.4 0.5 %collective-permute-start.6 = (bf16[32,2048]{1,0:T(8,128)(2,1)S(1)}, bf16[32,2048]{1,0:T(8,128)(2,1)S(1)}, u32[]{:S(2)}, u32[]{:S(2)}) collective-permute-start(bf16[32,2048]{1,0:T(8,128)(2,1)S(1)} %merge.3.own_ref), channel_id=1, source_target_pairs={{0,1},{1,0},{2,3},{3,2},{4,5},{5,4},{6,7},{7,6},{8,9},{9,8},{10,11... | collective-permute-start | bytes 393224 | tf_op jit(solution)/shard_map/ppermute | solution.py:229
  22.9 1.0 %collective-permute-done.6.got_ref = bf16[32,2048]{1,0:T(8,128)(2,1)S(1)} collective-permute-done((bf16[32,2048]{1,0:T(8,128)(2,1)S(1)}, bf16[32,2048]{1,0:T(8,128)(2,1)S(1)}, u32[]{:S(2)}, u32[]{:S(2)}) %collective-permute-start.6) | collective-permute-done | bytes 131104 | tf_op jit(solution)/shard_map/ppermute | solution.py:229
  24.0 1.9 %latent_stage.1 = (f32[32,2048]{1,0:T(8,128)S(1)}, bf16[32,2048]{1,0:T(8,128)(2,1)S(1)}) custom-call(s32[7,8,128]{2,1,0:T(8,128)S(1)} %place.1.flags_ref, bf16[64,2048]{1,0:T(8,128)(2,1)S(1)} %unite.1.gathered_ref, bf16[3,3,2048,128]{3,2,1,0:T(8,128)(2,1)S(1)} %bitcast.6, bf16[3,3,128,2048]{3,2,1,0:T(8,128)(2,1)S(1)} %bitcast.8), custom_call_target="tpu_custom_call" | custom-call | flops 603979776 | bytes 10223616 | tf_op jit(solution)/shard_map/latent_stage/pallas_call | solution.py:217
  25.9 0.4 %collective-permute-start.7 = (bf16[32,2048]{1,0:T(8,128)(2,1)S(1)}, bf16[32,2048]{1,0:T(8,128)(2,1)S(1)}, u32[]{:S(2)}, u32[]{:S(2)}) collective-permute-start(bf16[32,2048]{1,0:T(8,128)(2,1)S(1)} %get-tuple-element.14), channel_id=1, source_target_pairs={{0,1},{1,0},{2,3},{3,2},{4,5},{5,4},{6,7},{7,6},{8,9},{9,8},{10,11... | collective-permute-start | bytes 393224 | tf_op jit(solution)/shard_map/ppermute | solution.py:229
  26.3 1.0 %collective-permute-done.7.got_ref = bf16[32,2048]{1,0:T(8,128)(2,1)S(1)} collective-permute-done((bf16[32,2048]{1,0:T(8,128)(2,1)S(1)}, bf16[32,2048]{1,0:T(8,128)(2,1)S(1)}, u32[]{:S(2)}, u32[]{:S(2)}) %collective-permute-start.7) | collective-permute-done | bytes 131104 | tf_op jit(solution)/shard_map/ppermute | solution.py:229
  27.4 0.5 %collective-permute-start.8 = (bf16[16,2048]{1,0:T(8,128)(2,1)S(1)}, bf16[16,2048]{1,0:T(8,128)(2,1)S(1)}, u32[]{:S(2)}, u32[]{:S(2)}) collective-permute-start(bf16[16,2048]{1,0:T(8,128)(2,1)S(1)} %get-tuple-element.16), channel_id=1, source_target_pairs={{0,3},{1,2},{2,1},{3,0},{4,7},{5,6},{6,5},{7,4},{8,11},{9,10},{10,... | collective-permute-start | bytes 196616 | tf_op jit(solution)/shard_map/ppermute | solution.py:229
  27.9 3.4 %collective-permute-done.8.got_ref = bf16[16,2048]{1,0:T(8,128)(2,1)S(1)} collective-permute-done((bf16[16,2048]{1,0:T(8,128)(2,1)S(1)}, bf16[16,2048]{1,0:T(8,128)(2,1)S(1)}, u32[]{:S(2)}, u32[]{:S(2)}) %collective-permute-start.8) | collective-permute-done | bytes 65568 | tf_op jit(solution)/shard_map/ppermute | solution.py:229
  31.4 1.0 %collective-permute-start.9 = (bf16[4,2048]{1,0:T(4,128)(2,1)S(1)}, bf16[4,2048]{1,0:T(4,128)(2,1)S(1)}, u32[]{:S(2)}, u32[]{:S(2)}) collective-permute-start(bf16[4,2048]{1,0:T(4,128)(2,1)S(1)} %get-tuple-element.18), channel_id=1, source_target_pairs={{0,4},{1,5},{2,6},{3,7},{4,0},{5,1},{6,2},{7,3},{8,12},{9,13},{10,... | collective-permute-start | bytes 49160 | tf_op jit(solution)/shard_map/ppermute | solution.py:229
  32.3 1.6 %collective-permute-start.10 = (bf16[4,2048]{1,0:T(4,128)(2,1)S(1)}, bf16[4,2048]{1,0:T(4,128)(2,1)S(1)}, u32[]{:S(2)}, u32[]{:S(2)}) collective-permute-start(bf16[4,2048]{1,0:T(4,128)(2,1)S(1)} %get-tuple-element.19), channel_id=1, source_target_pairs={{0,9},{1,8},{2,11},{3,10},{4,13},{5,12},{6,15},{7,14},{8,1},{9,0},... | collective-permute-start | bytes 49160 | tf_op jit(solution)/shard_map/ppermute | solution.py:229
  33.9 1.6 %collective-permute-start.11 = (bf16[4,2048]{1,0:T(4,128)(2,1)S(1)}, bf16[4,2048]{1,0:T(4,128)(2,1)S(1)}, u32[]{:S(2)}, u32[]{:S(2)}) collective-permute-start(bf16[4,2048]{1,0:T(4,128)(2,1)S(1)} %get-tuple-element.20), channel_id=1, source_target_pairs={{0,13},{1,12},{2,15},{3,14},{4,9},{5,8},{6,11},{7,10},{8,5},{9,4},... | collective-permute-start | bytes 49160 | tf_op jit(solution)/shard_map/ppermute | solution.py:229
  35.5 1.0 %collective-permute-done.10 = bf16[4,2048]{1,0:T(4,128)(2,1)S(1)} collective-permute-done((bf16[4,2048]{1,0:T(4,128)(2,1)S(1)}, bf16[4,2048]{1,0:T(4,128)(2,1)S(1)}, u32[]{:S(2)}, u32[]{:S(2)}) %collective-permute-start.10) | collective-permute-done | bytes 16416 | tf_op jit(solution)/shard_map/ppermute | solution.py:229
  36.5 2.4 %collective-permute-done.11 = bf16[4,2048]{1,0:T(4,128)(2,1)S(1)} collective-permute-done((bf16[4,2048]{1,0:T(4,128)(2,1)S(1)}, bf16[4,2048]{1,0:T(4,128)(2,1)S(1)}, u32[]{:S(2)}, u32[]{:S(2)}) %collective-permute-start.11) | collective-permute-done | bytes 16416 | tf_op jit(solution)/shard_map/ppermute | solution.py:229
  38.9 0.6 %fusion = bf16[1,4,2048]{2,1,0:T(4,128)(2,1)} fusion(bf16[4,2048]{1,0:T(4,128)(2,1)S(1)} %collective-permute-done.11, bf16[4,2048]{1,0:T(4,128)(2,1)S(1)} %collective-permute-done.10, f32[4,2048]{1,0:T(4,128)S(1)} %get-tuple-element.17, bf16[4,2048]{1,0:T(4,128)(2,1)S(1)} %collective-permute-done.9, bf16[1,4,2048]{2,1,0:T(4,128)(2,1)S(1)} %image_stage.1), kind=kLoop, calls=%fused_computation.1 | loop fusion | flops 73728 | bytes 114688 | tf_op jit(solution)/shard_map/convert_element_type | solution.py:365
  (26 shorter events, 0.8 us)
Async XLA Ops:
  0.0 1.6 %collective-permute-start = (bf16[4,16,512]{2,1,0:T(8,128)(2,1)}, bf16[4,16,512]{2,1,0:T(8,128)(2,1)S(1)}, u32[]{:S(2)}, u32[]{:S(2)}) collective-permute-start(bf16[4,16,512]{2,1,0:T(8,128)(2,1)} %pixels_ref.1), channel_id=1, source_target_pairs={{0,1},{2,3},{4,5},{6,7},{8,9},{10,11},{12,13},{14,15},{1,0},{3,2},... | collective-permute-start | bytes 196616 | tf_op jit(solution)/shard_map/ppermute | solution.py:236
  0.5 1.1 %collective-permute-start.1 = (bf16[4,16,512]{2,1,0:T(8,128)(2,1)}, bf16[4,16,512]{2,1,0:T(8,128)(2,1)S(1)}, u32[]{:S(2)}, u32[]{:S(2)}) collective-permute-start(bf16[4,16,512]{2,1,0:T(8,128)(2,1)} %pixels_ref.1), channel_id=1, source_target_pairs={{1,2},{3,4},{5,6},{7,8},{9,10},{11,12},{13,14},{2,1},{4,3},{6,5},{... | collective-permute-start | bytes 196616 | tf_op jit(solution)/shard_map/ppermute | solution.py:235
  1.2 2.3 %copy-start = (bf16[3,3,512,512]{3,2,1,0:T(8,128)(2,1)S(1)}, bf16[3,3,512,512]{3,2,1,0:T(8,128)(2,1)}, u32[]{:S(2)}) copy-start(bf16[3,3,512,512]{3,2,1,0:T(8,128)(2,1)} %first_ref.1) | copy-start | bytes 14155780
  1.2 3.8 %copy-start.1 = (bf16[3,3,512,512]{3,2,1,0:T(8,128)(2,1)S(1)}, bf16[3,3,512,512]{3,2,1,0:T(8,128)(2,1)}, u32[]{:S(2)}) copy-start(bf16[3,3,512,512]{3,2,1,0:T(8,128)(2,1)} %second_ref.1) | copy-start | bytes 14155780
  1.2 3.8 %copy-start.2 = (bf16[4,16,512]{2,1,0:T(8,128)(2,1)S(1)}, bf16[4,16,512]{2,1,0:T(8,128)(2,1)}, u32[]{:S(2)}) copy-start(bf16[4,16,512]{2,1,0:T(8,128)(2,1)} %pixels_ref.1) | copy-start | bytes 196612
  7.1 16.8 %slice-start = ((s8[4718592]{0:T(1024)(128)(4,1)}), s8[4194304]{0:T(1024)(128)(4,1)S(1)}, s32[]{:S(2)}) async-start(s8[4718592]{0:T(1024)(128)(4,1)} %bitcast.5), calls=%async_computation | async-start | bytes 8388608
  7.1 16.8 %slice-start.2 = ((s8[4718592]{0:T(1024)(128)(4,1)}), s8[4194304]{0:T(1024)(128)(4,1)S(1)}, s32[]{:S(2)}) async-start(s8[4718592]{0:T(1024)(128)(4,1)} %bitcast.7), calls=%async_computation.2 | async-start | bytes 8388608
  7.2 16.8 %slice-start.1 = ((s8[4718592]{0:T(1024)(128)(4,1)}), s8[524288]{0:T(1024)(128)(4,1)S(1)}, s32[]{:S(2)}) async-start(s8[4718592]{0:T(1024)(128)(4,1)} %bitcast.5), calls=%async_computation.1 | async-start | bytes 1048576
  7.2 16.8 %slice-start.3 = ((s8[4718592]{0:T(1024)(128)(4,1)}), s8[524288]{0:T(1024)(128)(4,1)S(1)}, s32[]{:S(2)}) async-start(s8[4718592]{0:T(1024)(128)(4,1)} %bitcast.7), calls=%async_computation.3 | async-start | bytes 1048576
  7.2 8.6 %collective-permute-start.4 = (bf16[4,2048]{1,0:T(4,128)(2,1)S(1)}, bf16[4,2048]{1,0:T(4,128)(2,1)S(1)}, u32[]{:S(2)}, u32[]{:S(2)}) collective-permute-start(bf16[4,2048]{1,0:T(4,128)(2,1)S(1)} %bitcast.9), channel_id=1, source_target_pairs={{0,13},{1,12},{2,15},{3,14},{4,9},{5,8},{6,11},{7,10},{8,5},{9,4},... | collective-permute-start | bytes 49160 | tf_op jit(solution)/shard_map/ppermute | solution.py:229
  14.3 4.1 %collective-permute-start.3 = (bf16[4,2048]{1,0:T(4,128)(2,1)S(1)}, bf16[4,2048]{1,0:T(4,128)(2,1)S(1)}, u32[]{:S(2)}, u32[]{:S(2)}) collective-permute-start(bf16[4,2048]{1,0:T(4,128)(2,1)S(1)} %bitcast.10), channel_id=1, source_target_pairs={{0,9},{1,8},{2,11},{3,10},{4,13},{5,12},{6,15},{7,14},{8,1},{9,0},... | collective-permute-start | bytes 49160 | tf_op jit(solution)/shard_map/ppermute | solution.py:229
  14.3 4.1 %collective-permute-start.2 = (bf16[4,2048]{1,0:T(4,128)(2,1)S(1)}, bf16[4,2048]{1,0:T(4,128)(2,1)S(1)}, u32[]{:S(2)}, u32[]{:S(2)}) collective-permute-start(bf16[4,2048]{1,0:T(4,128)(2,1)S(1)} %bitcast.11), channel_id=1, source_target_pairs={{0,4},{1,5},{2,6},{3,7},{4,0},{5,1},{6,2},{7,3},{8,12},{9,13},{10,... | collective-permute-start | bytes 49160 | tf_op jit(solution)/shard_map/ppermute | solution.py:229
  18.4 3.9 %collective-permute-start.5 = (bf16[16,2048]{1,0:T(8,128)(2,1)S(1)}, bf16[16,2048]{1,0:T(8,128)(2,1)S(1)}, u32[]{:S(2)}, u32[]{:S(2)}) collective-permute-start(bf16[16,2048]{1,0:T(8,128)(2,1)S(1)} %merge.2.refs_0_), channel_id=1, source_target_pairs={{0,3},{1,2},{2,1},{3,0},{4,7},{5,6},{6,5},{7,4},{8,11},{9,10},{10,... | collective-permute-start | bytes 196616 | tf_op jit(solution)/shard_map/ppermute | solution.py:229
  22.4 1.4 %collective-permute-start.6 = (bf16[32,2048]{1,0:T(8,128)(2,1)S(1)}, bf16[32,2048]{1,0:T(8,128)(2,1)S(1)}, u32[]{:S(2)}, u32[]{:S(2)}) collective-permute-start(bf16[32,2048]{1,0:T(8,128)(2,1)S(1)} %merge.3.own_ref), channel_id=1, source_target_pairs={{0,1},{1,0},{2,3},{3,2},{4,5},{5,4},{6,7},{7,6},{8,9},{9,8},{10,11... | collective-permute-start | bytes 393224 | tf_op jit(solution)/shard_map/ppermute | solution.py:229
  25.9 1.4 %collective-permute-start.7 = (bf16[32,2048]{1,0:T(8,128)(2,1)S(1)}, bf16[32,2048]{1,0:T(8,128)(2,1)S(1)}, u32[]{:S(2)}, u32[]{:S(2)}) collective-permute-start(bf16[32,2048]{1,0:T(8,128)(2,1)S(1)} %get-tuple-element.14), channel_id=1, source_target_pairs={{0,1},{1,0},{2,3},{3,2},{4,5},{5,4},{6,7},{7,6},{8,9},{9,8},{10,11... | collective-permute-start | bytes 393224 | tf_op jit(solution)/shard_map/ppermute | solution.py:229
  27.4 3.9 %collective-permute-start.8 = (bf16[16,2048]{1,0:T(8,128)(2,1)S(1)}, bf16[16,2048]{1,0:T(8,128)(2,1)S(1)}, u32[]{:S(2)}, u32[]{:S(2)}) collective-permute-start(bf16[16,2048]{1,0:T(8,128)(2,1)S(1)} %get-tuple-element.16), channel_id=1, source_target_pairs={{0,3},{1,2},{2,1},{3,0},{4,7},{5,6},{6,5},{7,4},{8,11},{9,10},{10,... | collective-permute-start | bytes 196616 | tf_op jit(solution)/shard_map/ppermute | solution.py:229
  31.4 4.2 %collective-permute-start.9 = (bf16[4,2048]{1,0:T(4,128)(2,1)S(1)}, bf16[4,2048]{1,0:T(4,128)(2,1)S(1)}, u32[]{:S(2)}, u32[]{:S(2)}) collective-permute-start(bf16[4,2048]{1,0:T(4,128)(2,1)S(1)} %get-tuple-element.18), channel_id=1, source_target_pairs={{0,4},{1,5},{2,6},{3,7},{4,0},{5,1},{6,2},{7,3},{8,12},{9,13},{10,... | collective-permute-start | bytes 49160 | tf_op jit(solution)/shard_map/ppermute | solution.py:229
  32.3 4.2 %collective-permute-start.10 = (bf16[4,2048]{1,0:T(4,128)(2,1)S(1)}, bf16[4,2048]{1,0:T(4,128)(2,1)S(1)}, u32[]{:S(2)}, u32[]{:S(2)}) collective-permute-start(bf16[4,2048]{1,0:T(4,128)(2,1)S(1)} %get-tuple-element.19), channel_id=1, source_target_pairs={{0,9},{1,8},{2,11},{3,10},{4,13},{5,12},{6,15},{7,14},{8,1},{9,0},... | collective-permute-start | bytes 49160 | tf_op jit(solution)/shard_map/ppermute | solution.py:229
  33.9 5.0 %collective-permute-start.11 = (bf16[4,2048]{1,0:T(4,128)(2,1)S(1)}, bf16[4,2048]{1,0:T(4,128)(2,1)S(1)}, u32[]{:S(2)}, u32[]{:S(2)}) collective-permute-start(bf16[4,2048]{1,0:T(4,128)(2,1)S(1)} %get-tuple-element.20), channel_id=1, source_target_pairs={{0,13},{1,12},{2,15},{3,14},{4,9},{5,8},{6,11},{7,10},{8,5},{9,4},... | collective-permute-start | bytes 49160 | tf_op jit(solution)/shard_map/ppermute | solution.py:229

commit v2 on v1

--- a/solution.py
+++ b/solution.py
@@ -93,6 +93,8 @@
     edge = 2 * width
     before = pick(odd, inner[-edge:], outer[-edge:]).astype(BF16)
     after = pick(odd, outer[:edge], inner[:edge]).astype(BF16)
+    before = jnp.where(flag_of(flags_ref, bits), 0.0, before.astype(F32)).astype(BF16)
+    after = jnp.where(flag_of(flags_ref, bits + 1), 0.0, after.astype(F32)).astype(BF16)
     extended = jnp.concatenate([before, pixels, after], axis=0)
     activated = silu(conv_image(extended, first_ref, width)).astype(BF16).astype(F32)
     row = lax.broadcasted_iota(jnp.int32, activated.shape, 0) // width
@@ -229,12 +231,21 @@
     return lax.ppermute(value, "rows", [(i, i ^ bit) for i in range(peers)])
 
 
-def halo(value, peers):
-    pairs = [(i, i + 1) for i in range(0, peers - 1, 2)], [(i, i + 1) for i in range(1, peers - 1, 2)]
-    both = [one + [(j, i) for i, j in one] for one in pairs]
-    outer = lax.ppermute(value, "rows", both[1])
-    inner = lax.ppermute(value, "rows", both[0])
-    return inner, outer
+def halo(value, peers, groups):
+    got = []
+    for first in (0, 1):
+        partner = {}
+        for i in range(first, peers - 1, 2):
+            partner[i], partner[i + 1] = i + 1, i
+        pairs = []
+        for group in range(groups):
+            for i in range(peers):
+                if i in partner:
+                    pairs.append((group * peers + i, group * peers + partner[i]))
+                elif group ^ 1 < groups:
+                    pairs.append((group * peers + i, (group ^ 1) * peers + i))
+        got.append(lax.ppermute(value, ("groups", "rows"), pairs))
+    return got
 
 
 def merge_kernel(index, inner, flags_ref, *refs):
@@ -354,7 +365,7 @@
     peers = lax.axis_size("rows")
     me = lax.axis_index("rows")
     flags = placed(me, peers)
-    inner, outer = halo(pixels, peers)
+    inner, outer = halo(pixels, peers, lax.axis_size("groups"))
     latent = image_stage(flags, inner, outer, pixels, weight_first, weight_second)
     if peers != LINE * LOW or latent.shape[0] != 1 or weight_mix.shape[3] % LANES:
         return plain_latent(latent, weight_mix, weight_out)

time: 39.8 us -> 37.8 us (0.950)
  local copies, waits for them, and re-layouts: 3.37 us -> 1.35 us
  waiting for transfers between devices: 15.7 us -> 16.6 us
  starting transfers between devices: 15.2 us -> 14.4 us
    ppermute x10, starting transfers between devices: 14 us -> 11.5 us  [swap(): return lax.ppermute(value, 'rows', [(i, i ^ bit) for i in range(peers)])]
    ppermute x2, waiting for transfers between devices: 0.39 us -> 2.42 us  [halo(): got.append(lax.ppermute(value, ('groups', 'rows'), pairs))]
    unnamed x14, local copies, waits for them, and re-layouts: 3.37 us -> 1.35 us
    ppermute x2, starting transfers between devices: 1.15 us -> 2.97 us  [halo(): got.append(lax.ppermute(value, ('groups', 'rows'), pairs))]
    ppermute x10, waiting for transfers between devices: 15.3 us -> 14.2 us  [swap(): return lax.ppermute(value, 'rows', [(i, i ^ bit) for i in range(peers)])]
where the time goes in v2:
time: 37.8 us; the launch traced here: 37.6 us
  waiting for transfers between devices  16.6 us (44%)
  starting transfers between devices  14.4 us (38%)
  Pallas kernels  4.42 us (12%)
  local copies, waits for them, and re-layouts  1.35 us (4%)
  other arithmetic  0.63 us (2%)
    ppermute x10, waiting for transfers between devices, swap(): return lax.ppermute(value, 'rows', [(i, i ^ bit) for i in range(peers)])  14.2 us
    ppermute x10, starting transfers between devices, swap(): return lax.ppermute(value, 'rows', [(i, i ^ bit) for i in range(peers)])  11.5 us
    ppermute x2, starting transfers between devices, halo(): got.append(lax.ppermute(value, ('groups', 'rows'), pairs))  2.97 us
    ppermute x2, waiting for transfers between devices, halo(): got.append(lax.ppermute(value, ('groups', 'rows'), pairs))  2.42 us
    pallas_call x1, Pallas kernels, image_stage(): pl.pallas_call(image_kernel, out_shape=jax.ShapeDtypeStruct((rows // 4, w...  2.2 us
    pallas_call x1, Pallas kernels, latent_stage(): pl.pallas_call(functools.partial(latent_kernel, cols), out_shape=[jax.Sha...  1.86 us
    unnamed x14, local copies, waits for them, and re-layouts  1.35 us
  transfers between devices with their start and end apart: 12, of which 9 were waited for; matrix products, arithmetic and copies ran while one was open for 0% of the time, Pallas kernels for 0%

profile of v2, /device:TPU:0, one launch (start us, length us, event | category | flops | bytes accessed | tf_op | source)
XLA Modules:
  0.0 37.6 jit_solution(10747206570275536651)
XLA Ops:
  0.0 0.5 %collective-permute-start = (bf16[4,16,512]{2,1,0:T(8,128)(2,1)}, bf16[4,16,512]{2,1,0:T(8,128)(2,1)S(1)}, u32[]{:S(2)}, u32[]{:S(2)}) collective-permute-start(bf16[4,16,512]{2,1,0:T(8,128)(2,1)} %pixels_ref.1), channel_id=1, source_target_pairs={{0,1},{1,0},{2,3},{3,2},{4,5},{5,4},{6,7},{7,6},{8,9},{9,8},{10,11... | collective-permute-start | bytes 196616 | tf_op jit(solution)/shard_map/ppermute | solution.py:247
  0.5 2.5 %collective-permute-start.1 = (bf16[4,16,512]{2,1,0:T(8,128)(2,1)}, bf16[4,16,512]{2,1,0:T(8,128)(2,1)S(1)}, u32[]{:S(2)}, u32[]{:S(2)}) collective-permute-start(bf16[4,16,512]{2,1,0:T(8,128)(2,1)} %pixels_ref.1), channel_id=1, source_target_pairs={{0,16},{1,2},{2,1},{3,4},{4,3},{5,6},{6,5},{7,8},{8,7},{9,10},{10,... | collective-permute-start | bytes 196616 | tf_op jit(solution)/shard_map/ppermute | solution.py:247
  3.0 2.4 %collective-permute-done.1.outer_ref = bf16[4,16,512]{2,1,0:T(8,128)(2,1)S(1)} collective-permute-done((bf16[4,16,512]{2,1,0:T(8,128)(2,1)}, bf16[4,16,512]{2,1,0:T(8,128)(2,1)S(1)}, u32[]{:S(2)}, u32[]{:S(2)}) %collective-permute-start.1) | collective-permute-done | bytes 65568 | tf_op jit(solution)/shard_map/ppermute | solution.py:247
  5.4 1.3 %copy-done.1 = bf16[3,3,512,512]{3,2,1,0:T(8,128)(2,1)S(1)} copy-done((bf16[3,3,512,512]{3,2,1,0:T(8,128)(2,1)S(1)}, bf16[3,3,512,512]{3,2,1,0:T(8,128)(2,1)}, u32[]{:S(2)}) %copy-start.1) | copy-done | bytes 4718616
  6.8 2.2 %image_stage.1 = bf16[1,4,2048]{2,1,0:T(4,128)(2,1)S(1)} custom-call(s32[7,8,128]{2,1,0:T(8,128)S(1)} %place.1.flags_ref, bf16[4,16,512]{2,1,0:T(8,128)(2,1)S(1)} %collective-permute-done.inner_ref, bf16[4,16,512]{2,1,0:T(8,128)(2,1)S(1)} %collective-permute-done.1.outer_ref, bf16[4,16,512]{2,1,0:T(8,128)(2,1)S(1)} %copy-done.2, ...), custom_call_target="tpu_custom_call" | custom-call | flops 754974720 | bytes 9633792 | tf_op jit(solution)/shard_map/image_stage/pallas_call | solution.py:134
  9.0 3.4 %collective-permute-start.4 = (bf16[4,2048]{1,0:T(4,128)(2,1)S(1)}, bf16[4,2048]{1,0:T(4,128)(2,1)S(1)}, u32[]{:S(2)}, u32[]{:S(2)}) collective-permute-start(bf16[4,2048]{1,0:T(4,128)(2,1)S(1)} %bitcast.9), channel_id=1, source_target_pairs={{0,13},{1,12},{2,15},{3,14},{4,9},{5,8},{6,11},{7,10},{8,5},{9,4},... | collective-permute-start | bytes 49160 | tf_op jit(solution)/shard_map/ppermute | solution.py:231
  12.4 0.8 %collective-permute-start.2 = (bf16[4,2048]{1,0:T(4,128)(2,1)S(1)}, bf16[4,2048]{1,0:T(4,128)(2,1)S(1)}, u32[]{:S(2)}, u32[]{:S(2)}) collective-permute-start(bf16[4,2048]{1,0:T(4,128)(2,1)S(1)} %bitcast.11), channel_id=1, source_target_pairs={{0,4},{1,5},{2,6},{3,7},{4,0},{5,1},{6,2},{7,3},{8,12},{9,13},{10,... | collective-permute-start | bytes 49160 | tf_op jit(solution)/shard_map/ppermute | solution.py:231
  13.1 0.9 %collective-permute-done.4.refs_3_ = bf16[4,2048]{1,0:T(4,128)(2,1)S(1)} collective-permute-done((bf16[4,2048]{1,0:T(4,128)(2,1)S(1)}, bf16[4,2048]{1,0:T(4,128)(2,1)S(1)}, u32[]{:S(2)}, u32[]{:S(2)}) %collective-permute-start.4) | collective-permute-done | bytes 16416 | tf_op jit(solution)/shard_map/ppermute | solution.py:231
  14.0 2.5 %collective-permute-done.3.refs_2_ = bf16[4,2048]{1,0:T(4,128)(2,1)S(1)} collective-permute-done((bf16[4,2048]{1,0:T(4,128)(2,1)S(1)}, bf16[4,2048]{1,0:T(4,128)(2,1)S(1)}, u32[]{:S(2)}, u32[]{:S(2)}) %collective-permute-start.3) | collective-permute-done | bytes 16416 | tf_op jit(solution)/shard_map/ppermute | solution.py:231
  16.5 0.7 %collective-permute-start.5 = (bf16[16,2048]{1,0:T(8,128)(2,1)S(1)}, bf16[16,2048]{1,0:T(8,128)(2,1)S(1)}, u32[]{:S(2)}, u32[]{:S(2)}) collective-permute-start(bf16[16,2048]{1,0:T(8,128)(2,1)S(1)} %merge.2.refs_0_), channel_id=1, source_target_pairs={{0,3},{1,2},{2,1},{3,0},{4,7},{5,6},{6,5},{7,4},{8,11},{9,10},{10,... | collective-permute-start | bytes 196616 | tf_op jit(solution)/shard_map/ppermute | solution.py:231
  17.2 3.2 %collective-permute-done.5.refs_1_ = bf16[16,2048]{1,0:T(8,128)(2,1)S(1)} collective-permute-done((bf16[16,2048]{1,0:T(8,128)(2,1)S(1)}, bf16[16,2048]{1,0:T(8,128)(2,1)S(1)}, u32[]{:S(2)}, u32[]{:S(2)}) %collective-permute-start.5) | collective-permute-done | bytes 65568 | tf_op jit(solution)/shard_map/ppermute | solution.py:231
  20.5 0.5 %collective-permute-start.6 = (bf16[32,2048]{1,0:T(8,128)(2,1)S(1)}, bf16[32,2048]{1,0:T(8,128)(2,1)S(1)}, u32[]{:S(2)}, u32[]{:S(2)}) collective-permute-start(bf16[32,2048]{1,0:T(8,128)(2,1)S(1)} %merge.3.own_ref), channel_id=1, source_target_pairs={{0,1},{1,0},{2,3},{3,2},{4,5},{5,4},{6,7},{7,6},{8,9},{9,8},{10,11... | collective-permute-start | bytes 393224 | tf_op jit(solution)/shard_map/ppermute | solution.py:231
  20.9 1.0 %collective-permute-done.6.got_ref = bf16[32,2048]{1,0:T(8,128)(2,1)S(1)} collective-permute-done((bf16[32,2048]{1,0:T(8,128)(2,1)S(1)}, bf16[32,2048]{1,0:T(8,128)(2,1)S(1)}, u32[]{:S(2)}, u32[]{:S(2)}) %collective-permute-start.6) | collective-permute-done | bytes 131104 | tf_op jit(solution)/shard_map/ppermute | solution.py:231
  22.1 1.9 %latent_stage.1 = (f32[32,2048]{1,0:T(8,128)S(1)}, bf16[32,2048]{1,0:T(8,128)(2,1)S(1)}) custom-call(s32[7,8,128]{2,1,0:T(8,128)S(1)} %place.1.flags_ref, bf16[64,2048]{1,0:T(8,128)(2,1)S(1)} %unite.1.gathered_ref, bf16[3,3,2048,128]{3,2,1,0:T(8,128)(2,1)S(1)} %bitcast.6, bf16[3,3,128,2048]{3,2,1,0:T(8,128)(2,1)S(1)} %bitcast.8), custom_call_target="tpu_custom_call" | custom-call | flops 603979776 | bytes 10223616 | tf_op jit(solution)/shard_map/latent_stage/pallas_call | solution.py:219
  24.0 0.4 %collective-permute-start.7 = (bf16[32,2048]{1,0:T(8,128)(2,1)S(1)}, bf16[32,2048]{1,0:T(8,128)(2,1)S(1)}, u32[]{:S(2)}, u32[]{:S(2)}) collective-permute-start(bf16[32,2048]{1,0:T(8,128)(2,1)S(1)} %get-tuple-element.14), channel_id=1, source_target_pairs={{0,1},{1,0},{2,3},{3,2},{4,5},{5,4},{6,7},{7,6},{8,9},{9,8},{10,11... | collective-permute-start | bytes 393224 | tf_op jit(solution)/shard_map/ppermute | solution.py:231
  24.4 1.0 %collective-permute-done.7.got_ref = bf16[32,2048]{1,0:T(8,128)(2,1)S(1)} collective-permute-done((bf16[32,2048]{1,0:T(8,128)(2,1)S(1)}, bf16[32,2048]{1,0:T(8,128)(2,1)S(1)}, u32[]{:S(2)}, u32[]{:S(2)}) %collective-permute-start.7) | collective-permute-done | bytes 131104 | tf_op jit(solution)/shard_map/ppermute | solution.py:231
  25.5 1.6 %collective-permute-start.8 = (bf16[16,2048]{1,0:T(8,128)(2,1)S(1)}, bf16[16,2048]{1,0:T(8,128)(2,1)S(1)}, u32[]{:S(2)}, u32[]{:S(2)}) collective-permute-start(bf16[16,2048]{1,0:T(8,128)(2,1)S(1)} %get-tuple-element.16), channel_id=1, source_target_pairs={{0,3},{1,2},{2,1},{3,0},{4,7},{5,6},{6,5},{7,4},{8,11},{9,10},{10,... | collective-permute-start | bytes 196616 | tf_op jit(solution)/shard_map/ppermute | solution.py:231
  27.0 2.4 %collective-permute-done.8.got_ref = bf16[16,2048]{1,0:T(8,128)(2,1)S(1)} collective-permute-done((bf16[16,2048]{1,0:T(8,128)(2,1)S(1)}, bf16[16,2048]{1,0:T(8,128)(2,1)S(1)}, u32[]{:S(2)}, u32[]{:S(2)}) %collective-permute-start.8) | collective-permute-done | bytes 65568 | tf_op jit(solution)/shard_map/ppermute | solution.py:231
  29.4 1.2 %collective-permute-start.9 = (bf16[4,2048]{1,0:T(4,128)(2,1)S(1)}, bf16[4,2048]{1,0:T(4,128)(2,1)S(1)}, u32[]{:S(2)}, u32[]{:S(2)}) collective-permute-start(bf16[4,2048]{1,0:T(4,128)(2,1)S(1)} %get-tuple-element.18), channel_id=1, source_target_pairs={{0,4},{1,5},{2,6},{3,7},{4,0},{5,1},{6,2},{7,3},{8,12},{9,13},{10,... | collective-permute-start | bytes 49160 | tf_op jit(solution)/shard_map/ppermute | solution.py:231
  30.6 1.3 %collective-permute-start.10 = (bf16[4,2048]{1,0:T(4,128)(2,1)S(1)}, bf16[4,2048]{1,0:T(4,128)(2,1)S(1)}, u32[]{:S(2)}, u32[]{:S(2)}) collective-permute-start(bf16[4,2048]{1,0:T(4,128)(2,1)S(1)} %get-tuple-element.19), channel_id=1, source_target_pairs={{0,9},{1,8},{2,11},{3,10},{4,13},{5,12},{6,15},{7,14},{8,1},{9,0},... | collective-permute-start | bytes 49160 | tf_op jit(solution)/shard_map/ppermute | solution.py:231
  32.0 1.6 %collective-permute-start.11 = (bf16[4,2048]{1,0:T(4,128)(2,1)S(1)}, bf16[4,2048]{1,0:T(4,128)(2,1)S(1)}, u32[]{:S(2)}, u32[]{:S(2)}) collective-permute-start(bf16[4,2048]{1,0:T(4,128)(2,1)S(1)} %get-tuple-element.20), channel_id=1, source_target_pairs={{0,13},{1,12},{2,15},{3,14},{4,9},{5,8},{6,11},{7,10},{8,5},{9,4},... | collective-permute-start | bytes 49160 | tf_op jit(solution)/shard_map/ppermute | solution.py:231
  33.6 1.2 %collective-permute-done.10 = bf16[4,2048]{1,0:T(4,128)(2,1)S(1)} collective-permute-done((bf16[4,2048]{1,0:T(4,128)(2,1)S(1)}, bf16[4,2048]{1,0:T(4,128)(2,1)S(1)}, u32[]{:S(2)}, u32[]{:S(2)}) %collective-permute-start.10) | collective-permute-done | bytes 16416 | tf_op jit(solution)/shard_map/ppermute | solution.py:231
  34.8 2.1 %collective-permute-done.11 = bf16[4,2048]{1,0:T(4,128)(2,1)S(1)} collective-permute-done((bf16[4,2048]{1,0:T(4,128)(2,1)S(1)}, bf16[4,2048]{1,0:T(4,128)(2,1)S(1)}, u32[]{:S(2)}, u32[]{:S(2)}) %collective-permute-start.11) | collective-permute-done | bytes 16416 | tf_op jit(solution)/shard_map/ppermute | solution.py:231
  36.9 0.6 %fusion = bf16[1,4,2048]{2,1,0:T(4,128)(2,1)} fusion(bf16[4,2048]{1,0:T(4,128)(2,1)S(1)} %collective-permute-done.11, bf16[4,2048]{1,0:T(4,128)(2,1)S(1)} %collective-permute-done.10, f32[4,2048]{1,0:T(4,128)S(1)} %get-tuple-element.17, bf16[4,2048]{1,0:T(4,128)(2,1)S(1)} %collective-permute-done.9, bf16[1,4,2048]{2,1,0:T(4,128)(2,1)S(1)} %image_stage.1), kind=kLoop, calls=%fused_computation.1 | loop fusion | flops 73728 | bytes 114688 | tf_op jit(solution)/shard_map/convert_element_type | solution.py:376
  (26 shorter events, 0.4 us)
Async XLA Ops:
  0.0 3.0 %collective-permute-start = (bf16[4,16,512]{2,1,0:T(8,128)(2,1)}, bf16[4,16,512]{2,1,0:T(8,128)(2,1)S(1)}, u32[]{:S(2)}, u32[]{:S(2)}) collective-permute-start(bf16[4,16,512]{2,1,0:T(8,128)(2,1)} %pixels_ref.1), channel_id=1, source_target_pairs={{0,1},{1,0},{2,3},{3,2},{4,5},{5,4},{6,7},{7,6},{8,9},{9,8},{10,11... | collective-permute-start | bytes 196616 | tf_op jit(solution)/shard_map/ppermute | solution.py:247
  0.5 4.9 %collective-permute-start.1 = (bf16[4,16,512]{2,1,0:T(8,128)(2,1)}, bf16[4,16,512]{2,1,0:T(8,128)(2,1)S(1)}, u32[]{:S(2)}, u32[]{:S(2)}) collective-permute-start(bf16[4,16,512]{2,1,0:T(8,128)(2,1)} %pixels_ref.1), channel_id=1, source_target_pairs={{0,16},{1,2},{2,1},{3,4},{4,3},{5,6},{6,5},{7,8},{8,7},{9,10},{10,... | collective-permute-start | bytes 196616 | tf_op jit(solution)/shard_map/ppermute | solution.py:247
  3.0 2.5 %copy-start = (bf16[3,3,512,512]{3,2,1,0:T(8,128)(2,1)S(1)}, bf16[3,3,512,512]{3,2,1,0:T(8,128)(2,1)}, u32[]{:S(2)}) copy-start(bf16[3,3,512,512]{3,2,1,0:T(8,128)(2,1)} %first_ref.1) | copy-start | bytes 14155780
  3.0 3.8 %copy-start.1 = (bf16[3,3,512,512]{3,2,1,0:T(8,128)(2,1)S(1)}, bf16[3,3,512,512]{3,2,1,0:T(8,128)(2,1)}, u32[]{:S(2)}) copy-start(bf16[3,3,512,512]{3,2,1,0:T(8,128)(2,1)} %second_ref.1) | copy-start | bytes 14155780
  3.0 3.8 %copy-start.2 = (bf16[4,16,512]{2,1,0:T(8,128)(2,1)S(1)}, bf16[4,16,512]{2,1,0:T(8,128)(2,1)}, u32[]{:S(2)}) copy-start(bf16[4,16,512]{2,1,0:T(8,128)(2,1)} %pixels_ref.1) | copy-start | bytes 196612
  8.9 13.1 %slice-start = ((s8[4718592]{0:T(1024)(128)(4,1)}), s8[4194304]{0:T(1024)(128)(4,1)S(1)}, s32[]{:S(2)}) async-start(s8[4718592]{0:T(1024)(128)(4,1)} %bitcast.5), calls=%async_computation | async-start | bytes 8388608
  9.0 13.1 %slice-start.2 = ((s8[4718592]{0:T(1024)(128)(4,1)}), s8[4194304]{0:T(1024)(128)(4,1)S(1)}, s32[]{:S(2)}) async-start(s8[4718592]{0:T(1024)(128)(4,1)} %bitcast.7), calls=%async_computation.2 | async-start | bytes 8388608
  9.0 13.1 %slice-start.1 = ((s8[4718592]{0:T(1024)(128)(4,1)}), s8[524288]{0:T(1024)(128)(4,1)S(1)}, s32[]{:S(2)}) async-start(s8[4718592]{0:T(1024)(128)(4,1)} %bitcast.5), calls=%async_computation.1 | async-start | bytes 1048576
  9.0 13.1 %slice-start.3 = ((s8[4718592]{0:T(1024)(128)(4,1)}), s8[524288]{0:T(1024)(128)(4,1)S(1)}, s32[]{:S(2)}) async-start(s8[4718592]{0:T(1024)(128)(4,1)} %bitcast.7), calls=%async_computation.3 | async-start | bytes 1048576
  9.0 5.0 %collective-permute-start.4 = (bf16[4,2048]{1,0:T(4,128)(2,1)S(1)}, bf16[4,2048]{1,0:T(4,128)(2,1)S(1)}, u32[]{:S(2)}, u32[]{:S(2)}) collective-permute-start(bf16[4,2048]{1,0:T(4,128)(2,1)S(1)} %bitcast.9), channel_id=1, source_target_pairs={{0,13},{1,12},{2,15},{3,14},{4,9},{5,8},{6,11},{7,10},{8,5},{9,4},... | collective-permute-start | bytes 49160 | tf_op jit(solution)/shard_map/ppermute | solution.py:231
  12.4 4.1 %collective-permute-start.3 = (bf16[4,2048]{1,0:T(4,128)(2,1)S(1)}, bf16[4,2048]{1,0:T(4,128)(2,1)S(1)}, u32[]{:S(2)}, u32[]{:S(2)}) collective-permute-start(bf16[4,2048]{1,0:T(4,128)(2,1)S(1)} %bitcast.10), channel_id=1, source_target_pairs={{0,9},{1,8},{2,11},{3,10},{4,13},{5,12},{6,15},{7,14},{8,1},{9,0},... | collective-permute-start | bytes 49160 | tf_op jit(solution)/shard_map/ppermute | solution.py:231
  12.4 4.1 %collective-permute-start.2 = (bf16[4,2048]{1,0:T(4,128)(2,1)S(1)}, bf16[4,2048]{1,0:T(4,128)(2,1)S(1)}, u32[]{:S(2)}, u32[]{:S(2)}) collective-permute-start(bf16[4,2048]{1,0:T(4,128)(2,1)S(1)} %bitcast.11), channel_id=1, source_target_pairs={{0,4},{1,5},{2,6},{3,7},{4,0},{5,1},{6,2},{7,3},{8,12},{9,13},{10,... | collective-permute-start | bytes 49160 | tf_op jit(solution)/shard_map/ppermute | solution.py:231
  16.5 3.9 %collective-permute-start.5 = (bf16[16,2048]{1,0:T(8,128)(2,1)S(1)}, bf16[16,2048]{1,0:T(8,128)(2,1)S(1)}, u32[]{:S(2)}, u32[]{:S(2)}) collective-permute-start(bf16[16,2048]{1,0:T(8,128)(2,1)S(1)} %merge.2.refs_0_), channel_id=1, source_target_pairs={{0,3},{1,2},{2,1},{3,0},{4,7},{5,6},{6,5},{7,4},{8,11},{9,10},{10,... | collective-permute-start | bytes 196616 | tf_op jit(solution)/shard_map/ppermute | solution.py:231
  20.5 1.4 %collective-permute-start.6 = (bf16[32,2048]{1,0:T(8,128)(2,1)S(1)}, bf16[32,2048]{1,0:T(8,128)(2,1)S(1)}, u32[]{:S(2)}, u32[]{:S(2)}) collective-permute-start(bf16[32,2048]{1,0:T(8,128)(2,1)S(1)} %merge.3.own_ref), channel_id=1, source_target_pairs={{0,1},{1,0},{2,3},{3,2},{4,5},{5,4},{6,7},{7,6},{8,9},{9,8},{10,11... | collective-permute-start | bytes 393224 | tf_op jit(solution)/shard_map/ppermute | solution.py:231
  24.0 1.4 %collective-permute-start.7 = (bf16[32,2048]{1,0:T(8,128)(2,1)S(1)}, bf16[32,2048]{1,0:T(8,128)(2,1)S(1)}, u32[]{:S(2)}, u32[]{:S(2)}) collective-permute-start(bf16[32,2048]{1,0:T(8,128)(2,1)S(1)} %get-tuple-element.14), channel_id=1, source_target_pairs={{0,1},{1,0},{2,3},{3,2},{4,5},{5,4},{6,7},{7,6},{8,9},{9,8},{10,11... | collective-permute-start | bytes 393224 | tf_op jit(solution)/shard_map/ppermute | solution.py:231
  25.5 3.9 %collective-permute-start.8 = (bf16[16,2048]{1,0:T(8,128)(2,1)S(1)}, bf16[16,2048]{1,0:T(8,128)(2,1)S(1)}, u32[]{:S(2)}, u32[]{:S(2)}) collective-permute-start(bf16[16,2048]{1,0:T(8,128)(2,1)S(1)} %get-tuple-element.16), channel_id=1, source_target_pairs={{0,3},{1,2},{2,1},{3,0},{4,7},{5,6},{6,5},{7,4},{8,11},{9,10},{10,... | collective-permute-start | bytes 196616 | tf_op jit(solution)/shard_map/ppermute | solution.py:231
  29.4 4.2 %collective-permute-start.9 = (bf16[4,2048]{1,0:T(4,128)(2,1)S(1)}, bf16[4,2048]{1,0:T(4,128)(2,1)S(1)}, u32[]{:S(2)}, u32[]{:S(2)}) collective-permute-start(bf16[4,2048]{1,0:T(4,128)(2,1)S(1)} %get-tuple-element.18), channel_id=1, source_target_pairs={{0,4},{1,5},{2,6},{3,7},{4,0},{5,1},{6,2},{7,3},{8,12},{9,13},{10,... | collective-permute-start | bytes 49160 | tf_op jit(solution)/shard_map/ppermute | solution.py:231
  30.6 4.2 %collective-permute-start.10 = (bf16[4,2048]{1,0:T(4,128)(2,1)S(1)}, bf16[4,2048]{1,0:T(4,128)(2,1)S(1)}, u32[]{:S(2)}, u32[]{:S(2)}) collective-permute-start(bf16[4,2048]{1,0:T(4,128)(2,1)S(1)} %get-tuple-element.19), channel_id=1, source_target_pairs={{0,9},{1,8},{2,11},{3,10},{4,13},{5,12},{6,15},{7,14},{8,1},{9,0},... | collective-permute-start | bytes 49160 | tf_op jit(solution)/shard_map/ppermute | solution.py:231
  32.0 5.0 %collective-permute-start.11 = (bf16[4,2048]{1,0:T(4,128)(2,1)S(1)}, bf16[4,2048]{1,0:T(4,128)(2,1)S(1)}, u32[]{:S(2)}, u32[]{:S(2)}) collective-permute-start(bf16[4,2048]{1,0:T(4,128)(2,1)S(1)} %get-tuple-element.20), channel_id=1, source_target_pairs={{0,13},{1,12},{2,15},{3,14},{4,9},{5,8},{6,11},{7,10},{8,5},{9,4},... | collective-permute-start | bytes 49160 | tf_op jit(solution)/shard_map/ppermute | solution.py:231

commit v3 on v2

--- a/solution.py
+++ b/solution.py
@@ -35,22 +35,31 @@
     return core ^ (SIDE_FLIP * side) ^ (NEAR_FLIP * (place & 1)) ^ (FAR_FLIP * (place >> 1))
 
 
-def place_kernel(bits, last, me_ref, flags_ref):
+def place_kernel(bits, last, me_ref, flags_ref, spread_ref):
     me = me_ref[...]
     for bit in range(bits):
         flags_ref[bit] = (me >> bit) & 1
     flags_ref[bits] = (me == 0).astype(jnp.int32)
     flags_ref[bits + 1] = (me == last).astype(jnp.int32)
     flags_ref[bits + 2] = kind_of(me & 1, (me >> 1) & 1, (me >> 2) & 3)
+    shape = (LANES, spread_ref.shape[1])
+    source = lax.broadcasted_iota(jnp.int32, shape, 0)
+    target = lax.broadcasted_iota(jnp.int32, shape, 1)
+    for r in range(4):
+        place = target == 4 * source + 2 * (r % 2) + r // 2
+        spread_ref[r * LANES : (r + 1) * LANES] = place.astype(F32).astype(spread_ref.dtype)
 
 
 def placed(me, peers):
     bits = max(1, (peers - 1).bit_length())
     return pl.pallas_call(
         functools.partial(place_kernel, bits, peers - 1),
-        out_shape=jax.ShapeDtypeStruct((bits + 3, 8, LANES), jnp.int32),
+        out_shape=[
+            jax.ShapeDtypeStruct((bits + 3, 8, LANES), jnp.int32),
+            jax.ShapeDtypeStruct((4 * LANES, 4 * LANES), BF16),
+        ],
         in_specs=[VMEM],
-        out_specs=VMEM,
+        out_specs=[VMEM] * 2,
         compiler_params=pltpu.CompilerParams(vmem_limit_bytes=2 << 20),
         cost_estimate=pl.CostEstimate(flops=COVER, bytes_accessed=0, transcendentals=0),
         name="place",
@@ -70,7 +79,7 @@
 def conv_image(feature, weight_ref, width):
     out_rows = feature.shape[0] - 2 * width
     total = None
-    for col_tap in (1, 0, 2):
+    for col_tap in (0, 2, 1):
         term = None
         for row_tap in range(3):
             part = jnp.dot(
@@ -84,7 +93,12 @@
     return total
 
 
-def image_kernel(flags_ref, inner_ref, outer_ref, pixels_ref, first_ref, second_ref, latent_ref, wide_ref, packed_ref):
+def averaged(value_ref, chunk, count):
+    first, second = value_ref[chunk, pl.ds(0, count, stride=2), :], value_ref[chunk, pl.ds(1, count, stride=2), :]
+    return ((first + second) * 0.5).astype(BF16).astype(F32)
+
+
+def first_kernel(flags_ref, inner_ref, outer_ref, pixels_ref, first_ref, activated_ref):
     rows, width, chans = pixels_ref.shape
     flat = lambda ref: ref[...].reshape(ref.shape[0] * width, chans)
     pixels = flat(pixels_ref)
@@ -99,51 +113,64 @@
     activated = silu(conv_image(extended, first_ref, width)).astype(BF16).astype(F32)
     row = lax.broadcasted_iota(jnp.int32, activated.shape, 0) // width
     inside = (row >= flags_ref[bits, :1, :1]) & (row < rows + 2 - flags_ref[bits + 1, :1, :1])
-    activated = jnp.where(inside, activated, 0.0).astype(BF16)
-    block = pixels.astype(F32) + conv_image(activated, second_ref, width)
+    activated_ref[...] = jnp.where(inside, activated, 0.0).astype(BF16)
+
+
+def second_kernel(activated_ref, pixels_ref, spread_ref, second_ref, latent_ref, wide_ref, half_ref, packed_ref):
+    rows, width, chans = pixels_ref.shape
+    pixels = pixels_ref[...].reshape(rows * width, chans)
+    block = pixels.astype(F32) + conv_image(activated_ref[...], second_ref, width)
     block = block.astype(BF16).astype(F32)
     count = rows * width
-    half = ((block + pltpu.roll(block, count - 1, 0)) * 0.5).astype(BF16).astype(F32)
-    quarter = ((half + pltpu.roll(half, count - 2, 0)) * 0.5).astype(BF16).astype(F32)
     chunks = chans // LANES
     cols = width // 4
     for chunk in range(chunks):
-        wide_ref[chunk] = quarter[:, chunk * LANES : (chunk + 1) * LANES]
-    source = lax.broadcasted_iota(jnp.int32, (4 * LANES, 4 * LANES), 0)
-    target = lax.broadcasted_iota(jnp.int32, (4 * LANES, 4 * LANES), 1)
-    r = source // LANES
-    place = (target == 4 * (source % LANES) + 2 * (r % 2) + r // 2).astype(F32).astype(BF16)
+        wide_ref[chunk] = block[:, chunk * LANES : (chunk + 1) * LANES]
+    for chunk in range(chunks):
+        half_ref[chunk] = averaged(wide_ref, chunk, count // 2)
+    quarters = [averaged(half_ref, chunk, count // 4) for chunk in range(chunks)]
     for out_row in range(rows // 4):
         for chunk in range(chunks):
             for sub in range(4):
-                start = (4 * out_row + sub) * width
-                packed_ref[chunk * cols : (chunk + 1) * cols, sub * LANES : (sub + 1) * LANES] = wide_ref[
-                    chunk, pl.ds(start, cols, stride=4), :
+                start = (4 * out_row + sub) * cols
+                packed_ref[chunk * cols : (chunk + 1) * cols, sub * LANES : (sub + 1) * LANES] = quarters[chunk][
+                    start : start + cols
                 ]
-        spread = jnp.dot(packed_ref[...].astype(BF16), place, preferred_element_type=F32)
+        latent = jnp.dot(packed_ref[...].astype(BF16), spread_ref[...], preferred_element_type=F32)
         for chunk in range(chunks):
-            latent_ref[out_row, :, chunk * 4 * LANES : (chunk + 1) * 4 * LANES] = spread[
+            latent_ref[out_row, :, chunk * 4 * LANES : (chunk + 1) * 4 * LANES] = latent[
                 chunk * cols : (chunk + 1) * cols
             ].astype(BF16)
 
 
-def image_stage(flags, inner, outer, pixels, weight_first, weight_second):
+def image_stage(flags, spread, inner, outer, pixels, weight_first, weight_second):
     rows, width, chans = pixels.shape
-    flops = 2 * 9 * width * chans * chans * (2 * rows + 2)
-    moved = 2 * (weight_first.size + weight_second.size + 3 * pixels.size)
+    cost = lambda count, weight: pl.CostEstimate(
+        flops=2 * count * weight.size, bytes_accessed=2 * weight.size + 6 * pixels.size, transcendentals=0
+    )
+    activated = pl.pallas_call(
+        first_kernel,
+        out_shape=jax.ShapeDtypeStruct(((rows + 2) * width, chans), BF16),
+        in_specs=[VMEM] * 5,
+        out_specs=VMEM,
+        compiler_params=pltpu.CompilerParams(vmem_limit_bytes=16 << 20),
+        cost_estimate=cost((rows + 2) * width, weight_first),
+        name="first_stage",
+    )(flags, inner, outer, pixels, weight_first)
     return pl.pallas_call(
-        image_kernel,
+        second_kernel,
         out_shape=jax.ShapeDtypeStruct((rows // 4, width // 4, 4 * chans), BF16),
-        in_specs=[VMEM] * 6,
+        in_specs=[VMEM] * 4,
         out_specs=VMEM,
         scratch_shapes=[
             pltpu.VMEM((chans // LANES, rows * width, LANES), F32),
+            pltpu.VMEM((chans // LANES, rows * width // 2, LANES), F32),
             pltpu.VMEM((chans // LANES * (width // 4), 4 * LANES), F32),
         ],
-        compiler_params=pltpu.CompilerParams(vmem_limit_bytes=20 << 20),
-        cost_estimate=pl.CostEstimate(flops=flops, bytes_accessed=moved, transcendentals=rows * width * chans),
+        compiler_params=pltpu.CompilerParams(vmem_limit_bytes=16 << 20),
+        cost_estimate=cost(rows * width, weight_second),
         name="image_stage",
-    )(flags, inner, outer, pixels, weight_first, weight_second)
+    )(activated, pixels, spread, weight_second)
 
 
 def shift_rows(value, step, block, cols):
@@ -364,9 +391,9 @@
 def compute(pixels, weight_first, weight_second, weight_mix, weight_out):
     peers = lax.axis_size("rows")
     me = lax.axis_index("rows")
-    flags = placed(me, peers)
+    flags, spread = placed(me, peers)
     inner, outer = halo(pixels, peers, lax.axis_size("groups"))
-    latent = image_stage(flags, inner, outer, pixels, weight_first, weight_second)
+    latent = image_stage(flags, spread, inner, outer, pixels, weight_first, weight_second)
     if peers != LINE * LOW or latent.shape[0] != 1 or weight_mix.shape[3] % LANES:
         return plain_latent(latent, weight_mix, weight_out)
     cols = latent.shape[1]

time: 37.8 us -> 37.2 us (0.984)
  local copies, waits for them, and re-layouts: 1.35 us -> 0.49 us
  starting transfers between devices: 14.4 us -> 14.8 us
    unnamed x14 -> x16, local copies, waits for them, and re-layouts: 1.35 us -> 0.49 us
    pallas_call x1 -> x2, Pallas kernels: 2.2 us -> 2.08 us  [the longest x1 1.11 us: image_stage(): pl.pallas_call(second_kernel, out_shape=jax.ShapeDtypeStruct((rows // 4,...]
where the time goes in v3:
time: 37.2 us; the launch traced here: 37 us
  waiting for transfers between devices  16.6 us (45%)
  starting transfers between devices  14.8 us (40%)
  Pallas kernels  4.39 us (12%)
  other arithmetic  0.63 us (2%)
  local copies, waits for them, and re-layouts  0.49 us (1%)
    ppermute x10, waiting for transfers between devices, swap(): return lax.ppermute(value, 'rows', [(i, i ^ bit) for i in range(peers)])  14.4 us
    ppermute x10, starting transfers between devices, swap(): return lax.ppermute(value, 'rows', [(i, i ^ bit) for i in range(peers)])  11.7 us
    ppermute x2, starting transfers between devices, halo(): got.append(lax.ppermute(value, ('groups', 'rows'), pairs))  3.11 us
    ppermute x2, waiting for transfers between devices, halo(): got.append(lax.ppermute(value, ('groups', 'rows'), pairs))  2.18 us
    pallas_call x1, Pallas kernels, latent_stage(): pl.pallas_call(functools.partial(latent_kernel, cols), out_shape=[jax.Sha...  1.86 us
    pallas_call x1, Pallas kernels, image_stage(): pl.pallas_call(second_kernel, out_shape=jax.ShapeDtypeStruct((rows // 4,...  1.11 us
    pallas_call x1, Pallas kernels, image_stage(): pl.pallas_call(first_kernel, out_shape=jax.ShapeDtypeStruct(((rows + 2) *...  0.96 us
  transfers between devices with their start and end apart: 12, of which 9 were waited for; matrix products, arithmetic and copies ran while one was open for 0% of the time, Pallas kernels for 0%

profile of v3, /device:TPU:0, one launch (start us, length us, event | category | flops | bytes accessed | tf_op | source)
XLA Modules:
  0.0 37.0 jit_solution(17308107186140287487)
XLA Ops:
  0.0 3.0 %collective-permute-start.1 = (bf16[4,16,512]{2,1,0:T(8,128)(2,1)}, bf16[4,16,512]{2,1,0:T(8,128)(2,1)S(1)}, u32[]{:S(2)}, u32[]{:S(2)}) collective-permute-start(bf16[4,16,512]{2,1,0:T(8,128)(2,1)} %pixels_ref.3), channel_id=1, source_target_pairs={{0,16},{1,2},{2,1},{3,4},{4,3},{5,6},{6,5},{7,8},{8,7},{9,10},{10,... | collective-permute-start | bytes 196616 | tf_op jit(solution)/shard_map/ppermute | solution.py:274
  3.2 2.2 %collective-permute-done.1.outer_ref = bf16[4,16,512]{2,1,0:T(8,128)(2,1)S(1)} collective-permute-done((bf16[4,16,512]{2,1,0:T(8,128)(2,1)}, bf16[4,16,512]{2,1,0:T(8,128)(2,1)S(1)}, u32[]{:S(2)}, u32[]{:S(2)}) %collective-permute-start.1) | collective-permute-done | bytes 65568 | tf_op jit(solution)/shard_map/ppermute | solution.py:274
  5.4 0.2 copy-done
  5.6 1.0 %first_stage.1.activated_ref = bf16[96,512]{1,0:T(8,128)(2,1)S(1)} custom-call(s32[7,8,128]{2,1,0:T(8,128)S(1)} %get-tuple-element.15.flags_ref, bf16[4,16,512]{2,1,0:T(8,128)(2,1)S(1)} %collective-permute-done.inner_ref, bf16[4,16,512]{2,1,0:T(8,128)(2,1)S(1)} %collective-permute-done.1.outer_ref, bf16[4,16,512]{2,1,0:T(8,128)(2,1)S(1)} %copy-done.1, ...), custom_call_target="tpu_custom_call" | custom-call | flops 452984832 | bytes 4915200 | tf_op jit(solution)/shard_map/first_stage/pallas_call | solution.py:151
  6.9 1.1 %image_stage.1 = bf16[1,4,2048]{2,1,0:T(4,128)(2,1)S(1)} custom-call(bf16[96,512]{1,0:T(8,128)(2,1)S(1)} %first_stage.1.activated_ref, bf16[4,16,512]{2,1,0:T(8,128)(2,1)S(1)} %copy-done.1, bf16[512,512]{1,0:T(8,128)(2,1)S(1)} %get-tuple-element.16.spread_ref, bf16[3,3,512,512]{3,2,1,0:T(8,128)(2,1)S(1)} %bitcast.10), custom_call_target="tpu_custom_call" | custom-call | flops 301989888 | bytes 4915200 | tf_op jit(solution)/shard_map/image_stage/pallas_call | solution.py:160
  8.0 3.3 %collective-permute-start.4 = (bf16[4,2048]{1,0:T(4,128)(2,1)S(1)}, bf16[4,2048]{1,0:T(4,128)(2,1)S(1)}, u32[]{:S(2)}, u32[]{:S(2)}) collective-permute-start(bf16[4,2048]{1,0:T(4,128)(2,1)S(1)} %bitcast.11), channel_id=1, source_target_pairs={{0,13},{1,12},{2,15},{3,14},{4,9},{5,8},{6,11},{7,10},{8,5},{9,4},... | collective-permute-start | bytes 49160 | tf_op jit(solution)/shard_map/ppermute | solution.py:258
  11.3 0.9 %collective-permute-start.2 = (bf16[4,2048]{1,0:T(4,128)(2,1)S(1)}, bf16[4,2048]{1,0:T(4,128)(2,1)S(1)}, u32[]{:S(2)}, u32[]{:S(2)}) collective-permute-start(bf16[4,2048]{1,0:T(4,128)(2,1)S(1)} %bitcast.13), channel_id=1, source_target_pairs={{0,4},{1,5},{2,6},{3,7},{4,0},{5,1},{6,2},{7,3},{8,12},{9,13},{10,... | collective-permute-start | bytes 49160 | tf_op jit(solution)/shard_map/ppermute | solution.py:258
  12.2 0.9 %collective-permute-done.4.refs_3_ = bf16[4,2048]{1,0:T(4,128)(2,1)S(1)} collective-permute-done((bf16[4,2048]{1,0:T(4,128)(2,1)S(1)}, bf16[4,2048]{1,0:T(4,128)(2,1)S(1)}, u32[]{:S(2)}, u32[]{:S(2)}) %collective-permute-start.4) | collective-permute-done | bytes 16416 | tf_op jit(solution)/shard_map/ppermute | solution.py:258
  13.0 2.3 %collective-permute-done.3.refs_2_ = bf16[4,2048]{1,0:T(4,128)(2,1)S(1)} collective-permute-done((bf16[4,2048]{1,0:T(4,128)(2,1)S(1)}, bf16[4,2048]{1,0:T(4,128)(2,1)S(1)}, u32[]{:S(2)}, u32[]{:S(2)}) %collective-permute-start.3) | collective-permute-done | bytes 16416 | tf_op jit(solution)/shard_map/ppermute | solution.py:258
  15.4 1.2 %collective-permute-start.5 = (bf16[16,2048]{1,0:T(8,128)(2,1)S(1)}, bf16[16,2048]{1,0:T(8,128)(2,1)S(1)}, u32[]{:S(2)}, u32[]{:S(2)}) collective-permute-start(bf16[16,2048]{1,0:T(8,128)(2,1)S(1)} %merge.2.refs_0_), channel_id=1, source_target_pairs={{0,3},{1,2},{2,1},{3,0},{4,7},{5,6},{6,5},{7,4},{8,11},{9,10},{10,... | collective-permute-start | bytes 196616 | tf_op jit(solution)/shard_map/ppermute | solution.py:258
  16.6 2.5 %collective-permute-done.5.refs_1_ = bf16[16,2048]{1,0:T(8,128)(2,1)S(1)} collective-permute-done((bf16[16,2048]{1,0:T(8,128)(2,1)S(1)}, bf16[16,2048]{1,0:T(8,128)(2,1)S(1)}, u32[]{:S(2)}, u32[]{:S(2)}) %collective-permute-start.5) | collective-permute-done | bytes 65568 | tf_op jit(solution)/shard_map/ppermute | solution.py:258
  19.3 1.0 %collective-permute-start.6 = (bf16[32,2048]{1,0:T(8,128)(2,1)S(1)}, bf16[32,2048]{1,0:T(8,128)(2,1)S(1)}, u32[]{:S(2)}, u32[]{:S(2)}) collective-permute-start(bf16[32,2048]{1,0:T(8,128)(2,1)S(1)} %merge.3.own_ref), channel_id=1, source_target_pairs={{0,1},{1,0},{2,3},{3,2},{4,5},{5,4},{6,7},{7,6},{8,9},{9,8},{10,11... | collective-permute-start | bytes 393224 | tf_op jit(solution)/shard_map/ppermute | solution.py:258
  20.3 1.0 %collective-permute-done.6.got_ref = bf16[32,2048]{1,0:T(8,128)(2,1)S(1)} collective-permute-done((bf16[32,2048]{1,0:T(8,128)(2,1)S(1)}, bf16[32,2048]{1,0:T(8,128)(2,1)S(1)}, u32[]{:S(2)}, u32[]{:S(2)}) %collective-permute-start.6) | collective-permute-done | bytes 131104 | tf_op jit(solution)/shard_map/ppermute | solution.py:258
  21.4 1.9 %latent_stage.1 = (f32[32,2048]{1,0:T(8,128)S(1)}, bf16[32,2048]{1,0:T(8,128)(2,1)S(1)}) custom-call(s32[7,8,128]{2,1,0:T(8,128)S(1)} %get-tuple-element.15.flags_ref, bf16[64,2048]{1,0:T(8,128)(2,1)S(1)} %unite.1.gathered_ref, bf16[3,3,2048,128]{3,2,1,0:T(8,128)(2,1)S(1)} %bitcast.6, bf16[3,3,128,2048]{3,2,1,0:T(8,128)(2,1)S(1)} %bitcast.8), custom_call_target="tpu_custom_call" | custom-call | flops 603979776 | bytes 10223616 | tf_op jit(solution)/shard_map/latent_stage/pallas_call | solution.py:246
  23.3 0.4 %collective-permute-start.7 = (bf16[32,2048]{1,0:T(8,128)(2,1)S(1)}, bf16[32,2048]{1,0:T(8,128)(2,1)S(1)}, u32[]{:S(2)}, u32[]{:S(2)}) collective-permute-start(bf16[32,2048]{1,0:T(8,128)(2,1)S(1)} %get-tuple-element.18), channel_id=1, source_target_pairs={{0,1},{1,0},{2,3},{3,2},{4,5},{5,4},{6,7},{7,6},{8,9},{9,8},{10,11... | collective-permute-start | bytes 393224 | tf_op jit(solution)/shard_map/ppermute | solution.py:258
  23.7 1.0 %collective-permute-done.7.got_ref = bf16[32,2048]{1,0:T(8,128)(2,1)S(1)} collective-permute-done((bf16[32,2048]{1,0:T(8,128)(2,1)S(1)}, bf16[32,2048]{1,0:T(8,128)(2,1)S(1)}, u32[]{:S(2)}, u32[]{:S(2)}) %collective-permute-start.7) | collective-permute-done | bytes 131104 | tf_op jit(solution)/shard_map/ppermute | solution.py:258
  24.8 0.7 %collective-permute-start.8 = (bf16[16,2048]{1,0:T(8,128)(2,1)S(1)}, bf16[16,2048]{1,0:T(8,128)(2,1)S(1)}, u32[]{:S(2)}, u32[]{:S(2)}) collective-permute-start(bf16[16,2048]{1,0:T(8,128)(2,1)S(1)} %get-tuple-element.20), channel_id=1, source_target_pairs={{0,3},{1,2},{2,1},{3,0},{4,7},{5,6},{6,5},{7,4},{8,11},{9,10},{10,... | collective-permute-start | bytes 196616 | tf_op jit(solution)/shard_map/ppermute | solution.py:258
  25.4 3.3 %collective-permute-done.8.got_ref = bf16[16,2048]{1,0:T(8,128)(2,1)S(1)} collective-permute-done((bf16[16,2048]{1,0:T(8,128)(2,1)S(1)}, bf16[16,2048]{1,0:T(8,128)(2,1)S(1)}, u32[]{:S(2)}, u32[]{:S(2)}) %collective-permute-start.8) | collective-permute-done | bytes 65568 | tf_op jit(solution)/shard_map/ppermute | solution.py:258
  28.7 0.8 %collective-permute-start.9 = (bf16[4,2048]{1,0:T(4,128)(2,1)S(1)}, bf16[4,2048]{1,0:T(4,128)(2,1)S(1)}, u32[]{:S(2)}, u32[]{:S(2)}) collective-permute-start(bf16[4,2048]{1,0:T(4,128)(2,1)S(1)} %get-tuple-element.22), channel_id=1, source_target_pairs={{0,4},{1,5},{2,6},{3,7},{4,0},{5,1},{6,2},{7,3},{8,12},{9,13},{10,... | collective-permute-start | bytes 49160 | tf_op jit(solution)/shard_map/ppermute | solution.py:258
  29.5 1.9 %collective-permute-start.10 = (bf16[4,2048]{1,0:T(4,128)(2,1)S(1)}, bf16[4,2048]{1,0:T(4,128)(2,1)S(1)}, u32[]{:S(2)}, u32[]{:S(2)}) collective-permute-start(bf16[4,2048]{1,0:T(4,128)(2,1)S(1)} %get-tuple-element.23), channel_id=1, source_target_pairs={{0,9},{1,8},{2,11},{3,10},{4,13},{5,12},{6,15},{7,14},{8,1},{9,0},... | collective-permute-start | bytes 49160 | tf_op jit(solution)/shard_map/ppermute | solution.py:258
  31.4 1.5 %collective-permute-start.11 = (bf16[4,2048]{1,0:T(4,128)(2,1)S(1)}, bf16[4,2048]{1,0:T(4,128)(2,1)S(1)}, u32[]{:S(2)}, u32[]{:S(2)}) collective-permute-start(bf16[4,2048]{1,0:T(4,128)(2,1)S(1)} %get-tuple-element.24), channel_id=1, source_target_pairs={{0,13},{1,12},{2,15},{3,14},{4,9},{5,8},{6,11},{7,10},{8,5},{9,4},... | collective-permute-start | bytes 49160 | tf_op jit(solution)/shard_map/ppermute | solution.py:258
  32.9 0.8 %collective-permute-done.10 = bf16[4,2048]{1,0:T(4,128)(2,1)S(1)} collective-permute-done((bf16[4,2048]{1,0:T(4,128)(2,1)S(1)}, bf16[4,2048]{1,0:T(4,128)(2,1)S(1)}, u32[]{:S(2)}, u32[]{:S(2)}) %collective-permute-start.10) | collective-permute-done | bytes 16416 | tf_op jit(solution)/shard_map/ppermute | solution.py:258
  33.7 2.7 %collective-permute-done.11 = bf16[4,2048]{1,0:T(4,128)(2,1)S(1)} collective-permute-done((bf16[4,2048]{1,0:T(4,128)(2,1)S(1)}, bf16[4,2048]{1,0:T(4,128)(2,1)S(1)}, u32[]{:S(2)}, u32[]{:S(2)}) %collective-permute-start.11) | collective-permute-done | bytes 16416 | tf_op jit(solution)/shard_map/ppermute | solution.py:258
  36.4 0.6 %fusion = bf16[1,4,2048]{2,1,0:T(4,128)(2,1)} fusion(bf16[4,2048]{1,0:T(4,128)(2,1)S(1)} %collective-permute-done.11, bf16[4,2048]{1,0:T(4,128)(2,1)S(1)} %collective-permute-done.10, f32[4,2048]{1,0:T(4,128)S(1)} %get-tuple-element.21, bf16[4,2048]{1,0:T(4,128)(2,1)S(1)} %collective-permute-done.9, bf16[1,4,2048]{2,1,0:T(4,128)(2,1)S(1)} %image_stage.1), kind=kLoop, calls=%fused_computation.1 | loop fusion | flops 73728 | bytes 114688 | tf_op jit(solution)/shard_map/convert_element_type | solution.py:403
  (30 shorter events, 0.9 us)
Async XLA Ops:
  0.0 5.4 %collective-permute-start.1 = (bf16[4,16,512]{2,1,0:T(8,128)(2,1)}, bf16[4,16,512]{2,1,0:T(8,128)(2,1)S(1)}, u32[]{:S(2)}, u32[]{:S(2)}) collective-permute-start(bf16[4,16,512]{2,1,0:T(8,128)(2,1)} %pixels_ref.3), channel_id=1, source_target_pairs={{0,16},{1,2},{2,1},{3,4},{4,3},{5,6},{6,5},{7,8},{8,7},{9,10},{10,... | collective-permute-start | bytes 196616 | tf_op jit(solution)/shard_map/ppermute | solution.py:274
  3.0 2.5 %collective-permute-start = (bf16[4,16,512]{2,1,0:T(8,128)(2,1)}, bf16[4,16,512]{2,1,0:T(8,128)(2,1)S(1)}, u32[]{:S(2)}, u32[]{:S(2)}) collective-permute-start(bf16[4,16,512]{2,1,0:T(8,128)(2,1)} %pixels_ref.3), channel_id=1, source_target_pairs={{0,1},{1,0},{2,3},{3,2},{4,5},{5,4},{6,7},{7,6},{8,9},{9,8},{10,11... | collective-permute-start | bytes 196616 | tf_op jit(solution)/shard_map/ppermute | solution.py:274
  3.1 3.6 %slice-start.4 = ((s8[4718592]{0:T(1024)(128)(4,1)}), s8[4194304]{0:T(1024)(128)(4,1)S(1)}, s32[]{:S(2)}) async-start(s8[4718592]{0:T(1024)(128)(4,1)} %bitcast.9), calls=%async_computation.4 | async-start | bytes 8388608
  3.1 2.5 %copy-start = (bf16[3,3,512,512]{3,2,1,0:T(8,128)(2,1)S(1)}, bf16[3,3,512,512]{3,2,1,0:T(8,128)(2,1)}, u32[]{:S(2)}) copy-start(bf16[3,3,512,512]{3,2,1,0:T(8,128)(2,1)} %first_ref.1) | copy-start | bytes 14155780
  3.1 2.5 %copy-start.1 = (bf16[4,16,512]{2,1,0:T(8,128)(2,1)S(1)}, bf16[4,16,512]{2,1,0:T(8,128)(2,1)}, u32[]{:S(2)}) copy-start(bf16[4,16,512]{2,1,0:T(8,128)(2,1)} %pixels_ref.3) | copy-start | bytes 196612
  3.1 3.7 %slice-start.5 = ((s8[4718592]{0:T(1024)(128)(4,1)}), s8[524288]{0:T(1024)(128)(4,1)S(1)}, s32[]{:S(2)}) async-start(s8[4718592]{0:T(1024)(128)(4,1)} %bitcast.9), calls=%async_computation.5 | async-start | bytes 1048576
  8.0 13.4 %slice-start = ((s8[4718592]{0:T(1024)(128)(4,1)}), s8[4194304]{0:T(1024)(128)(4,1)S(1)}, s32[]{:S(2)}) async-start(s8[4718592]{0:T(1024)(128)(4,1)} %bitcast.5), calls=%async_computation | async-start | bytes 8388608
  8.0 13.4 %slice-start.2 = ((s8[4718592]{0:T(1024)(128)(4,1)}), s8[4194304]{0:T(1024)(128)(4,1)S(1)}, s32[]{:S(2)}) async-start(s8[4718592]{0:T(1024)(128)(4,1)} %bitcast.7), calls=%async_computation.2 | async-start | bytes 8388608
  8.0 13.4 %slice-start.1 = ((s8[4718592]{0:T(1024)(128)(4,1)}), s8[524288]{0:T(1024)(128)(4,1)S(1)}, s32[]{:S(2)}) async-start(s8[4718592]{0:T(1024)(128)(4,1)} %bitcast.5), calls=%async_computation.1 | async-start | bytes 1048576
  8.0 13.4 %slice-start.3 = ((s8[4718592]{0:T(1024)(128)(4,1)}), s8[524288]{0:T(1024)(128)(4,1)S(1)}, s32[]{:S(2)}) async-start(s8[4718592]{0:T(1024)(128)(4,1)} %bitcast.7), calls=%async_computation.3 | async-start | bytes 1048576
  8.0 5.0 %collective-permute-start.4 = (bf16[4,2048]{1,0:T(4,128)(2,1)S(1)}, bf16[4,2048]{1,0:T(4,128)(2,1)S(1)}, u32[]{:S(2)}, u32[]{:S(2)}) collective-permute-start(bf16[4,2048]{1,0:T(4,128)(2,1)S(1)} %bitcast.11), channel_id=1, source_target_pairs={{0,13},{1,12},{2,15},{3,14},{4,9},{5,8},{6,11},{7,10},{8,5},{9,4},... | collective-permute-start | bytes 49160 | tf_op jit(solution)/shard_map/ppermute | solution.py:258
  11.3 4.1 %collective-permute-start.3 = (bf16[4,2048]{1,0:T(4,128)(2,1)S(1)}, bf16[4,2048]{1,0:T(4,128)(2,1)S(1)}, u32[]{:S(2)}, u32[]{:S(2)}) collective-permute-start(bf16[4,2048]{1,0:T(4,128)(2,1)S(1)} %bitcast.12), channel_id=1, source_target_pairs={{0,9},{1,8},{2,11},{3,10},{4,13},{5,12},{6,15},{7,14},{8,1},{9,0},... | collective-permute-start | bytes 49160 | tf_op jit(solution)/shard_map/ppermute | solution.py:258
  11.3 4.1 %collective-permute-start.2 = (bf16[4,2048]{1,0:T(4,128)(2,1)S(1)}, bf16[4,2048]{1,0:T(4,128)(2,1)S(1)}, u32[]{:S(2)}, u32[]{:S(2)}) collective-permute-start(bf16[4,2048]{1,0:T(4,128)(2,1)S(1)} %bitcast.13), channel_id=1, source_target_pairs={{0,4},{1,5},{2,6},{3,7},{4,0},{5,1},{6,2},{7,3},{8,12},{9,13},{10,... | collective-permute-start | bytes 49160 | tf_op jit(solution)/shard_map/ppermute | solution.py:258
  15.4 3.8 %collective-permute-start.5 = (bf16[16,2048]{1,0:T(8,128)(2,1)S(1)}, bf16[16,2048]{1,0:T(8,128)(2,1)S(1)}, u32[]{:S(2)}, u32[]{:S(2)}) collective-permute-start(bf16[16,2048]{1,0:T(8,128)(2,1)S(1)} %merge.2.refs_0_), channel_id=1, source_target_pairs={{0,3},{1,2},{2,1},{3,0},{4,7},{5,6},{6,5},{7,4},{8,11},{9,10},{10,... | collective-permute-start | bytes 196616 | tf_op jit(solution)/shard_map/ppermute | solution.py:258
  19.3 2.0 %collective-permute-start.6 = (bf16[32,2048]{1,0:T(8,128)(2,1)S(1)}, bf16[32,2048]{1,0:T(8,128)(2,1)S(1)}, u32[]{:S(2)}, u32[]{:S(2)}) collective-permute-start(bf16[32,2048]{1,0:T(8,128)(2,1)S(1)} %merge.3.own_ref), channel_id=1, source_target_pairs={{0,1},{1,0},{2,3},{3,2},{4,5},{5,4},{6,7},{7,6},{8,9},{9,8},{10,11... | collective-permute-start | bytes 393224 | tf_op jit(solution)/shard_map/ppermute | solution.py:258
  23.3 1.4 %collective-permute-start.7 = (bf16[32,2048]{1,0:T(8,128)(2,1)S(1)}, bf16[32,2048]{1,0:T(8,128)(2,1)S(1)}, u32[]{:S(2)}, u32[]{:S(2)}) collective-permute-start(bf16[32,2048]{1,0:T(8,128)(2,1)S(1)} %get-tuple-element.18), channel_id=1, source_target_pairs={{0,1},{1,0},{2,3},{3,2},{4,5},{5,4},{6,7},{7,6},{8,9},{9,8},{10,11... | collective-permute-start | bytes 393224 | tf_op jit(solution)/shard_map/ppermute | solution.py:258
  24.8 3.9 %collective-permute-start.8 = (bf16[16,2048]{1,0:T(8,128)(2,1)S(1)}, bf16[16,2048]{1,0:T(8,128)(2,1)S(1)}, u32[]{:S(2)}, u32[]{:S(2)}) collective-permute-start(bf16[16,2048]{1,0:T(8,128)(2,1)S(1)} %get-tuple-element.20), channel_id=1, source_target_pairs={{0,3},{1,2},{2,1},{3,0},{4,7},{5,6},{6,5},{7,4},{8,11},{9,10},{10,... | collective-permute-start | bytes 196616 | tf_op jit(solution)/shard_map/ppermute | solution.py:258
  28.7 4.2 %collective-permute-start.9 = (bf16[4,2048]{1,0:T(4,128)(2,1)S(1)}, bf16[4,2048]{1,0:T(4,128)(2,1)S(1)}, u32[]{:S(2)}, u32[]{:S(2)}) collective-permute-start(bf16[4,2048]{1,0:T(4,128)(2,1)S(1)} %get-tuple-element.22), channel_id=1, source_target_pairs={{0,4},{1,5},{2,6},{3,7},{4,0},{5,1},{6,2},{7,3},{8,12},{9,13},{10,... | collective-permute-start | bytes 49160 | tf_op jit(solution)/shard_map/ppermute | solution.py:258
  29.5 4.2 %collective-permute-start.10 = (bf16[4,2048]{1,0:T(4,128)(2,1)S(1)}, bf16[4,2048]{1,0:T(4,128)(2,1)S(1)}, u32[]{:S(2)}, u32[]{:S(2)}) collective-permute-start(bf16[4,2048]{1,0:T(4,128)(2,1)S(1)} %get-tuple-element.23), channel_id=1, source_target_pairs={{0,9},{1,8},{2,11},{3,10},{4,13},{5,12},{6,15},{7,14},{8,1},{9,0},... | collective-permute-start | bytes 49160 | tf_op jit(solution)/shard_map/ppermute | solution.py:258
  31.4 5.0 %collective-permute-start.11 = (bf16[4,2048]{1,0:T(4,128)(2,1)S(1)}, bf16[4,2048]{1,0:T(4,128)(2,1)S(1)}, u32[]{:S(2)}, u32[]{:S(2)}) collective-permute-start(bf16[4,2048]{1,0:T(4,128)(2,1)S(1)} %get-tuple-element.24), channel_id=1, source_target_pairs={{0,13},{1,12},{2,15},{3,14},{4,9},{5,8},{6,11},{7,10},{8,5},{9,4},... | collective-permute-start | bytes 49160 | tf_op jit(solution)/shard_map/ppermute | solution.py:258

commit v4 on v3

--- a/solution.py
+++ b/solution.py
@@ -206,7 +206,8 @@
             send_ref[run * inner : (run + 1) * inner] = part.astype(send_ref.dtype)
 
 
-def latent_kernel(cols, flags_ref, gathered_ref, mix_ref, out_ref, keep_ref, send_ref):
+def latent_kernel(cols, flags_ref, own_ref, got_ref, mix_ref, out_ref, keep_ref, send_ref, gathered_ref):
+    unite_kernel(flags_ref, own_ref, got_ref, gathered_ref)
     feature = gathered_ref[...]
     block = feature.shape[0] // LOW
     hidden_count = mix_ref.shape[3]
@@ -239,19 +240,20 @@
         send_ref[index * cols : (index + 1) * cols] = pick(kind, first, second).astype(send_ref.dtype)
 
 
-def latent_stage(flags, gathered, weight_mix, weight_out, cols):
-    count, chans = gathered.shape
+def latent_stage(flags, own, got, weight_mix, weight_out, cols):
+    count, chans = 2 * own.shape[0], own.shape[1]
     flops = 2 * count * (weight_mix.size + weight_out.size)
-    moved = 2 * (weight_mix.size + weight_out.size) + 6 * gathered.size
+    moved = 2 * (weight_mix.size + weight_out.size) + 6 * count * chans
     return pl.pallas_call(
         functools.partial(latent_kernel, cols),
         out_shape=[jax.ShapeDtypeStruct((count // 2, chans), kind) for kind in (F32, BF16)],
-        in_specs=[VMEM] * 4,
+        in_specs=[VMEM] * 5,
         out_specs=[VMEM] * 2,
+        scratch_shapes=[pltpu.VMEM((count, chans), BF16)],
         compiler_params=pltpu.CompilerParams(vmem_limit_bytes=20 << 20),
         cost_estimate=pl.CostEstimate(flops=flops, bytes_accessed=moved, transcendentals=count * weight_mix.shape[3]),
         name="latent_stage",
-    )(flags, gathered, weight_mix, weight_out)
+    )(flags, own, got, weight_mix, weight_out)
 
 
 def swap(value, peers, bit):
@@ -301,19 +303,6 @@
             both_ref[start : start + cols] = block.astype(both_ref.dtype)
 
 
-def united(flags, own, got):
-    rows, chans = own.shape
-    return pl.pallas_call(
-        unite_kernel,
-        out_shape=jax.ShapeDtypeStruct((2 * rows, chans), own.dtype),
-        in_specs=[VMEM] * 3,
-        out_specs=VMEM,
-        compiler_params=pltpu.CompilerParams(vmem_limit_bytes=2 << 20),
-        cost_estimate=pl.CostEstimate(flops=0, bytes_accessed=8 * own.size, transcendentals=0),
-        name="unite",
-    )(flags, own, got)
-
-
 def merged(flags, blocks, index, inner, cover=0):
     rows, chans = blocks[0].shape
     return pl.pallas_call(
@@ -337,7 +326,7 @@
 def gather_rows(latent, flags, peers, cols):
     held = merged(flags, [latent, *exchanged([latent] * (LINE - 1), peers)], LOW.bit_length() - 1, cols, COVER)
     held = merged(flags, [held, swap(held, peers, 2 + SIDE_FLIP)], 1, held.shape[0])
-    return united(flags, held, swap(held, peers, 1))
+    return held, swap(held, peers, 1)
 
 
 def halve_kernel(index, inner, flags_ref, held_ref, got_ref, keep_ref, *send_refs):
@@ -397,8 +386,8 @@
     if peers != LINE * LOW or latent.shape[0] != 1 or weight_mix.shape[3] % LANES:
         return plain_latent(latent, weight_mix, weight_out)
     cols = latent.shape[1]
-    gathered = gather_rows(latent[0], flags, peers, cols)
-    keep, send = latent_stage(flags, gathered, weight_mix, weight_out, cols)
+    own, got = gather_rows(latent[0], flags, peers, cols)
+    keep, send = latent_stage(flags, own, got, weight_mix, weight_out, cols)
     mixed = scatter_sum(keep, send, flags, peers, cols)
     return (latent.astype(F32) + mixed[None]).astype(BF16)
 

time: 37.2 us -> 37.1 us (level)
  no operation moved by 1% of the time
where the time goes in v4:
time: 37.1 us; the launch traced here: 36.9 us
  waiting for transfers between devices  16.6 us (45%)
  starting transfers between devices  14.8 us (40%)
  Pallas kernels  4.35 us (12%)
  other arithmetic  0.63 us (2%)
  local copies, waits for them, and re-layouts  0.49 us (1%)
    ppermute x10, waiting for transfers between devices, swap(): return lax.ppermute(value, 'rows', [(i, i ^ bit) for i in range(peers)])  14.4 us
    ppermute x10, starting transfers between devices, swap(): return lax.ppermute(value, 'rows', [(i, i ^ bit) for i in range(peers)])  11.6 us
    ppermute x2, starting transfers between devices, halo(): got.append(lax.ppermute(value, ('groups', 'rows'), pairs))  3.11 us
    ppermute x2, waiting for transfers between devices, halo(): got.append(lax.ppermute(value, ('groups', 'rows'), pairs))  2.18 us
    pallas_call x1, Pallas kernels, latent_stage(): pl.pallas_call(functools.partial(latent_kernel, cols), out_shape=[jax.Sha...  1.93 us
    pallas_call x1, Pallas kernels, image_stage(): pl.pallas_call(second_kernel, out_shape=jax.ShapeDtypeStruct((rows // 4,...  1.11 us
    pallas_call x1, Pallas kernels, image_stage(): pl.pallas_call(first_kernel, out_shape=jax.ShapeDtypeStruct(((rows + 2) *...  0.96 us
  transfers between devices with their start and end apart: 12, of which 9 were waited for; matrix products, arithmetic and copies ran while one was open for 0% of the time, Pallas kernels for 0%

profile of v4, /device:TPU:0, one launch (start us, length us, event | category | flops | bytes accessed | tf_op | source)
XLA Modules:
  0.0 36.9 jit_solution(8616875228456132657)
XLA Ops:
  0.0 3.0 %collective-permute-start.1 = (bf16[4,16,512]{2,1,0:T(8,128)(2,1)}, bf16[4,16,512]{2,1,0:T(8,128)(2,1)S(1)}, u32[]{:S(2)}, u32[]{:S(2)}) collective-permute-start(bf16[4,16,512]{2,1,0:T(8,128)(2,1)} %pixels_ref.3), channel_id=1, source_target_pairs={{0,16},{1,2},{2,1},{3,4},{4,3},{5,6},{6,5},{7,8},{8,7},{9,10},{10,... | collective-permute-start | bytes 196616 | tf_op jit(solution)/shard_map/ppermute | solution.py:276
  3.2 2.2 %collective-permute-done.1.outer_ref = bf16[4,16,512]{2,1,0:T(8,128)(2,1)S(1)} collective-permute-done((bf16[4,16,512]{2,1,0:T(8,128)(2,1)}, bf16[4,16,512]{2,1,0:T(8,128)(2,1)S(1)}, u32[]{:S(2)}, u32[]{:S(2)}) %collective-permute-start.1) | collective-permute-done | bytes 65568 | tf_op jit(solution)/shard_map/ppermute | solution.py:276
  5.4 0.2 copy-done
  5.6 1.0 %first_stage.1.activated_ref = bf16[96,512]{1,0:T(8,128)(2,1)S(1)} custom-call(s32[7,8,128]{2,1,0:T(8,128)S(1)} %get-tuple-element.15.flags_ref, bf16[4,16,512]{2,1,0:T(8,128)(2,1)S(1)} %collective-permute-done.inner_ref, bf16[4,16,512]{2,1,0:T(8,128)(2,1)S(1)} %collective-permute-done.1.outer_ref, bf16[4,16,512]{2,1,0:T(8,128)(2,1)S(1)} %copy-done.1, ...), custom_call_target="tpu_custom_call" | custom-call | flops 452984832 | bytes 4915200 | tf_op jit(solution)/shard_map/first_stage/pallas_call | solution.py:151
  6.9 1.1 %image_stage.1 = bf16[1,4,2048]{2,1,0:T(4,128)(2,1)S(1)} custom-call(bf16[96,512]{1,0:T(8,128)(2,1)S(1)} %first_stage.1.activated_ref, bf16[4,16,512]{2,1,0:T(8,128)(2,1)S(1)} %copy-done.1, bf16[512,512]{1,0:T(8,128)(2,1)S(1)} %get-tuple-element.16.spread_ref, bf16[3,3,512,512]{3,2,1,0:T(8,128)(2,1)S(1)} %bitcast.10), custom_call_target="tpu_custom_call" | custom-call | flops 301989888 | bytes 4915200 | tf_op jit(solution)/shard_map/image_stage/pallas_call | solution.py:160
  8.0 3.3 %collective-permute-start.4 = (bf16[4,2048]{1,0:T(4,128)(2,1)S(1)}, bf16[4,2048]{1,0:T(4,128)(2,1)S(1)}, u32[]{:S(2)}, u32[]{:S(2)}) collective-permute-start(bf16[4,2048]{1,0:T(4,128)(2,1)S(1)} %bitcast.11), channel_id=1, source_target_pairs={{0,13},{1,12},{2,15},{3,14},{4,9},{5,8},{6,11},{7,10},{8,5},{9,4},... | collective-permute-start | bytes 49160 | tf_op jit(solution)/shard_map/ppermute | solution.py:260
  11.3 0.9 %collective-permute-start.2 = (bf16[4,2048]{1,0:T(4,128)(2,1)S(1)}, bf16[4,2048]{1,0:T(4,128)(2,1)S(1)}, u32[]{:S(2)}, u32[]{:S(2)}) collective-permute-start(bf16[4,2048]{1,0:T(4,128)(2,1)S(1)} %bitcast.13), channel_id=1, source_target_pairs={{0,4},{1,5},{2,6},{3,7},{4,0},{5,1},{6,2},{7,3},{8,12},{9,13},{10,... | collective-permute-start | bytes 49160 | tf_op jit(solution)/shard_map/ppermute | solution.py:260
  12.2 0.9 %collective-permute-done.4.refs_3_ = bf16[4,2048]{1,0:T(4,128)(2,1)S(1)} collective-permute-done((bf16[4,2048]{1,0:T(4,128)(2,1)S(1)}, bf16[4,2048]{1,0:T(4,128)(2,1)S(1)}, u32[]{:S(2)}, u32[]{:S(2)}) %collective-permute-start.4) | collective-permute-done | bytes 16416 | tf_op jit(solution)/shard_map/ppermute | solution.py:260
  13.0 2.3 %collective-permute-done.3.refs_2_ = bf16[4,2048]{1,0:T(4,128)(2,1)S(1)} collective-permute-done((bf16[4,2048]{1,0:T(4,128)(2,1)S(1)}, bf16[4,2048]{1,0:T(4,128)(2,1)S(1)}, u32[]{:S(2)}, u32[]{:S(2)}) %collective-permute-start.3) | collective-permute-done | bytes 16416 | tf_op jit(solution)/shard_map/ppermute | solution.py:260
  15.4 1.2 %collective-permute-start.5 = (bf16[16,2048]{1,0:T(8,128)(2,1)S(1)}, bf16[16,2048]{1,0:T(8,128)(2,1)S(1)}, u32[]{:S(2)}, u32[]{:S(2)}) collective-permute-start(bf16[16,2048]{1,0:T(8,128)(2,1)S(1)} %merge.2.refs_0_), channel_id=1, source_target_pairs={{0,3},{1,2},{2,1},{3,0},{4,7},{5,6},{6,5},{7,4},{8,11},{9,10},{10,... | collective-permute-start | bytes 196616 | tf_op jit(solution)/shard_map/ppermute | solution.py:260
  16.6 2.5 %collective-permute-done.5.refs_1_ = bf16[16,2048]{1,0:T(8,128)(2,1)S(1)} collective-permute-done((bf16[16,2048]{1,0:T(8,128)(2,1)S(1)}, bf16[16,2048]{1,0:T(8,128)(2,1)S(1)}, u32[]{:S(2)}, u32[]{:S(2)}) %collective-permute-start.5) | collective-permute-done | bytes 65568 | tf_op jit(solution)/shard_map/ppermute | solution.py:260
  19.3 1.0 %collective-permute-start.6 = (bf16[32,2048]{1,0:T(8,128)(2,1)S(1)}, bf16[32,2048]{1,0:T(8,128)(2,1)S(1)}, u32[]{:S(2)}, u32[]{:S(2)}) collective-permute-start(bf16[32,2048]{1,0:T(8,128)(2,1)S(1)} %merge.3.own_ref), channel_id=1, source_target_pairs={{0,1},{1,0},{2,3},{3,2},{4,5},{5,4},{6,7},{7,6},{8,9},{9,8},{10,11... | collective-permute-start | bytes 393224 | tf_op jit(solution)/shard_map/ppermute | solution.py:260
  20.3 1.0 %collective-permute-done.6.got_ref = bf16[32,2048]{1,0:T(8,128)(2,1)S(1)} collective-permute-done((bf16[32,2048]{1,0:T(8,128)(2,1)S(1)}, bf16[32,2048]{1,0:T(8,128)(2,1)S(1)}, u32[]{:S(2)}, u32[]{:S(2)}) %collective-permute-start.6) | collective-permute-done | bytes 131104 | tf_op jit(solution)/shard_map/ppermute | solution.py:260
  21.3 1.9 %latent_stage.1 = (f32[32,2048]{1,0:T(8,128)S(1)}, bf16[32,2048]{1,0:T(8,128)(2,1)S(1)}) custom-call(s32[7,8,128]{2,1,0:T(8,128)S(1)} %get-tuple-element.15.flags_ref, bf16[32,2048]{1,0:T(8,128)(2,1)S(1)} %merge.3.own_ref, bf16[32,2048]{1,0:T(8,128)(2,1)S(1)} %collective-permute-done.6.got_ref, bf16[3,3,2048,128]{3,2,1,0:T(8,128)(2,1)S(1)} %bitcast.6, ...), custom_call_target="tpu_custom_call" | custom-call | flops 603979776 | bytes 10223616 | tf_op jit(solution)/shard_map/latent_stage/pallas_call | solution.py:247
  23.2 0.4 %collective-permute-start.7 = (bf16[32,2048]{1,0:T(8,128)(2,1)S(1)}, bf16[32,2048]{1,0:T(8,128)(2,1)S(1)}, u32[]{:S(2)}, u32[]{:S(2)}) collective-permute-start(bf16[32,2048]{1,0:T(8,128)(2,1)S(1)} %get-tuple-element.18), channel_id=1, source_target_pairs={{0,1},{1,0},{2,3},{3,2},{4,5},{5,4},{6,7},{7,6},{8,9},{9,8},{10,11... | collective-permute-start | bytes 393224 | tf_op jit(solution)/shard_map/ppermute | solution.py:260
  23.6 1.0 %collective-permute-done.7.got_ref = bf16[32,2048]{1,0:T(8,128)(2,1)S(1)} collective-permute-done((bf16[32,2048]{1,0:T(8,128)(2,1)S(1)}, bf16[32,2048]{1,0:T(8,128)(2,1)S(1)}, u32[]{:S(2)}, u32[]{:S(2)}) %collective-permute-start.7) | collective-permute-done | bytes 131104 | tf_op jit(solution)/shard_map/ppermute | solution.py:260
  24.7 0.6 %collective-permute-start.8 = (bf16[16,2048]{1,0:T(8,128)(2,1)S(1)}, bf16[16,2048]{1,0:T(8,128)(2,1)S(1)}, u32[]{:S(2)}, u32[]{:S(2)}) collective-permute-start(bf16[16,2048]{1,0:T(8,128)(2,1)S(1)} %get-tuple-element.20), channel_id=1, source_target_pairs={{0,3},{1,2},{2,1},{3,0},{4,7},{5,6},{6,5},{7,4},{8,11},{9,10},{10,... | collective-permute-start | bytes 196616 | tf_op jit(solution)/shard_map/ppermute | solution.py:260
  25.3 3.3 %collective-permute-done.8.got_ref = bf16[16,2048]{1,0:T(8,128)(2,1)S(1)} collective-permute-done((bf16[16,2048]{1,0:T(8,128)(2,1)S(1)}, bf16[16,2048]{1,0:T(8,128)(2,1)S(1)}, u32[]{:S(2)}, u32[]{:S(2)}) %collective-permute-start.8) | collective-permute-done | bytes 65568 | tf_op jit(solution)/shard_map/ppermute | solution.py:260
  28.7 0.8 %collective-permute-start.9 = (bf16[4,2048]{1,0:T(4,128)(2,1)S(1)}, bf16[4,2048]{1,0:T(4,128)(2,1)S(1)}, u32[]{:S(2)}, u32[]{:S(2)}) collective-permute-start(bf16[4,2048]{1,0:T(4,128)(2,1)S(1)} %get-tuple-element.22), channel_id=1, source_target_pairs={{0,4},{1,5},{2,6},{3,7},{4,0},{5,1},{6,2},{7,3},{8,12},{9,13},{10,... | collective-permute-start | bytes 49160 | tf_op jit(solution)/shard_map/ppermute | solution.py:260
  29.5 1.9 %collective-permute-start.10 = (bf16[4,2048]{1,0:T(4,128)(2,1)S(1)}, bf16[4,2048]{1,0:T(4,128)(2,1)S(1)}, u32[]{:S(2)}, u32[]{:S(2)}) collective-permute-start(bf16[4,2048]{1,0:T(4,128)(2,1)S(1)} %get-tuple-element.23), channel_id=1, source_target_pairs={{0,9},{1,8},{2,11},{3,10},{4,13},{5,12},{6,15},{7,14},{8,1},{9,0},... | collective-permute-start | bytes 49160 | tf_op jit(solution)/shard_map/ppermute | solution.py:260
  31.3 1.5 %collective-permute-start.11 = (bf16[4,2048]{1,0:T(4,128)(2,1)S(1)}, bf16[4,2048]{1,0:T(4,128)(2,1)S(1)}, u32[]{:S(2)}, u32[]{:S(2)}) collective-permute-start(bf16[4,2048]{1,0:T(4,128)(2,1)S(1)} %get-tuple-element.24), channel_id=1, source_target_pairs={{0,13},{1,12},{2,15},{3,14},{4,9},{5,8},{6,11},{7,10},{8,5},{9,4},... | collective-permute-start | bytes 49160 | tf_op jit(solution)/shard_map/ppermute | solution.py:260
  32.8 0.8 %collective-permute-done.10 = bf16[4,2048]{1,0:T(4,128)(2,1)S(1)} collective-permute-done((bf16[4,2048]{1,0:T(4,128)(2,1)S(1)}, bf16[4,2048]{1,0:T(4,128)(2,1)S(1)}, u32[]{:S(2)}, u32[]{:S(2)}) %collective-permute-start.10) | collective-permute-done | bytes 16416 | tf_op jit(solution)/shard_map/ppermute | solution.py:260
  33.6 2.7 %collective-permute-done.11 = bf16[4,2048]{1,0:T(4,128)(2,1)S(1)} collective-permute-done((bf16[4,2048]{1,0:T(4,128)(2,1)S(1)}, bf16[4,2048]{1,0:T(4,128)(2,1)S(1)}, u32[]{:S(2)}, u32[]{:S(2)}) %collective-permute-start.11) | collective-permute-done | bytes 16416 | tf_op jit(solution)/shard_map/ppermute | solution.py:260
  36.3 0.6 %fusion = bf16[1,4,2048]{2,1,0:T(4,128)(2,1)} fusion(bf16[4,2048]{1,0:T(4,128)(2,1)S(1)} %collective-permute-done.11, bf16[4,2048]{1,0:T(4,128)(2,1)S(1)} %collective-permute-done.10, f32[4,2048]{1,0:T(4,128)S(1)} %get-tuple-element.21, bf16[4,2048]{1,0:T(4,128)(2,1)S(1)} %collective-permute-done.9, bf16[1,4,2048]{2,1,0:T(4,128)(2,1)S(1)} %image_stage.1), kind=kLoop, calls=%fused_computation.1 | loop fusion | flops 73728 | bytes 114688 | tf_op jit(solution)/shard_map/convert_element_type | solution.py:392
  (29 shorter events, 0.8 us)
Async XLA Ops:
  0.0 5.4 %collective-permute-start.1 = (bf16[4,16,512]{2,1,0:T(8,128)(2,1)}, bf16[4,16,512]{2,1,0:T(8,128)(2,1)S(1)}, u32[]{:S(2)}, u32[]{:S(2)}) collective-permute-start(bf16[4,16,512]{2,1,0:T(8,128)(2,1)} %pixels_ref.3), channel_id=1, source_target_pairs={{0,16},{1,2},{2,1},{3,4},{4,3},{5,6},{6,5},{7,8},{8,7},{9,10},{10,... | collective-permute-start | bytes 196616 | tf_op jit(solution)/shard_map/ppermute | solution.py:276
  3.0 2.5 %collective-permute-start = (bf16[4,16,512]{2,1,0:T(8,128)(2,1)}, bf16[4,16,512]{2,1,0:T(8,128)(2,1)S(1)}, u32[]{:S(2)}, u32[]{:S(2)}) collective-permute-start(bf16[4,16,512]{2,1,0:T(8,128)(2,1)} %pixels_ref.3), channel_id=1, source_target_pairs={{0,1},{1,0},{2,3},{3,2},{4,5},{5,4},{6,7},{7,6},{8,9},{9,8},{10,11... | collective-permute-start | bytes 196616 | tf_op jit(solution)/shard_map/ppermute | solution.py:276
  3.1 3.6 %slice-start.4 = ((s8[4718592]{0:T(1024)(128)(4,1)}), s8[4194304]{0:T(1024)(128)(4,1)S(1)}, s32[]{:S(2)}) async-start(s8[4718592]{0:T(1024)(128)(4,1)} %bitcast.9), calls=%async_computation.4 | async-start | bytes 8388608
  3.1 2.5 %copy-start = (bf16[3,3,512,512]{3,2,1,0:T(8,128)(2,1)S(1)}, bf16[3,3,512,512]{3,2,1,0:T(8,128)(2,1)}, u32[]{:S(2)}) copy-start(bf16[3,3,512,512]{3,2,1,0:T(8,128)(2,1)} %first_ref.1) | copy-start | bytes 14155780
  3.1 2.5 %copy-start.1 = (bf16[4,16,512]{2,1,0:T(8,128)(2,1)S(1)}, bf16[4,16,512]{2,1,0:T(8,128)(2,1)}, u32[]{:S(2)}) copy-start(bf16[4,16,512]{2,1,0:T(8,128)(2,1)} %pixels_ref.3) | copy-start | bytes 196612
  3.1 3.7 %slice-start.5 = ((s8[4718592]{0:T(1024)(128)(4,1)}), s8[524288]{0:T(1024)(128)(4,1)S(1)}, s32[]{:S(2)}) async-start(s8[4718592]{0:T(1024)(128)(4,1)} %bitcast.9), calls=%async_computation.5 | async-start | bytes 1048576
  8.0 13.3 %slice-start = ((s8[4718592]{0:T(1024)(128)(4,1)}), s8[4194304]{0:T(1024)(128)(4,1)S(1)}, s32[]{:S(2)}) async-start(s8[4718592]{0:T(1024)(128)(4,1)} %bitcast.5), calls=%async_computation | async-start | bytes 8388608
  8.0 13.3 %slice-start.2 = ((s8[4718592]{0:T(1024)(128)(4,1)}), s8[4194304]{0:T(1024)(128)(4,1)S(1)}, s32[]{:S(2)}) async-start(s8[4718592]{0:T(1024)(128)(4,1)} %bitcast.7), calls=%async_computation.2 | async-start | bytes 8388608
  8.0 13.3 %slice-start.1 = ((s8[4718592]{0:T(1024)(128)(4,1)}), s8[524288]{0:T(1024)(128)(4,1)S(1)}, s32[]{:S(2)}) async-start(s8[4718592]{0:T(1024)(128)(4,1)} %bitcast.5), calls=%async_computation.1 | async-start | bytes 1048576
  8.0 13.3 %slice-start.3 = ((s8[4718592]{0:T(1024)(128)(4,1)}), s8[524288]{0:T(1024)(128)(4,1)S(1)}, s32[]{:S(2)}) async-start(s8[4718592]{0:T(1024)(128)(4,1)} %bitcast.7), calls=%async_computation.3 | async-start | bytes 1048576
  8.0 5.0 %collective-permute-start.4 = (bf16[4,2048]{1,0:T(4,128)(2,1)S(1)}, bf16[4,2048]{1,0:T(4,128)(2,1)S(1)}, u32[]{:S(2)}, u32[]{:S(2)}) collective-permute-start(bf16[4,2048]{1,0:T(4,128)(2,1)S(1)} %bitcast.11), channel_id=1, source_target_pairs={{0,13},{1,12},{2,15},{3,14},{4,9},{5,8},{6,11},{7,10},{8,5},{9,4},... | collective-permute-start | bytes 49160 | tf_op jit(solution)/shard_map/ppermute | solution.py:260
  11.3 4.1 %collective-permute-start.3 = (bf16[4,2048]{1,0:T(4,128)(2,1)S(1)}, bf16[4,2048]{1,0:T(4,128)(2,1)S(1)}, u32[]{:S(2)}, u32[]{:S(2)}) collective-permute-start(bf16[4,2048]{1,0:T(4,128)(2,1)S(1)} %bitcast.12), channel_id=1, source_target_pairs={{0,9},{1,8},{2,11},{3,10},{4,13},{5,12},{6,15},{7,14},{8,1},{9,0},... | collective-permute-start | bytes 49160 | tf_op jit(solution)/shard_map/ppermute | solution.py:260
  11.3 4.1 %collective-permute-start.2 = (bf16[4,2048]{1,0:T(4,128)(2,1)S(1)}, bf16[4,2048]{1,0:T(4,128)(2,1)S(1)}, u32[]{:S(2)}, u32[]{:S(2)}) collective-permute-start(bf16[4,2048]{1,0:T(4,128)(2,1)S(1)} %bitcast.13), channel_id=1, source_target_pairs={{0,4},{1,5},{2,6},{3,7},{4,0},{5,1},{6,2},{7,3},{8,12},{9,13},{10,... | collective-permute-start | bytes 49160 | tf_op jit(solution)/shard_map/ppermute | solution.py:260
  15.4 3.8 %collective-permute-start.5 = (bf16[16,2048]{1,0:T(8,128)(2,1)S(1)}, bf16[16,2048]{1,0:T(8,128)(2,1)S(1)}, u32[]{:S(2)}, u32[]{:S(2)}) collective-permute-start(bf16[16,2048]{1,0:T(8,128)(2,1)S(1)} %merge.2.refs_0_), channel_id=1, source_target_pairs={{0,3},{1,2},{2,1},{3,0},{4,7},{5,6},{6,5},{7,4},{8,11},{9,10},{10,... | collective-permute-start | bytes 196616 | tf_op jit(solution)/shard_map/ppermute | solution.py:260
  19.3 2.0 %collective-permute-start.6 = (bf16[32,2048]{1,0:T(8,128)(2,1)S(1)}, bf16[32,2048]{1,0:T(8,128)(2,1)S(1)}, u32[]{:S(2)}, u32[]{:S(2)}) collective-permute-start(bf16[32,2048]{1,0:T(8,128)(2,1)S(1)} %merge.3.own_ref), channel_id=1, source_target_pairs={{0,1},{1,0},{2,3},{3,2},{4,5},{5,4},{6,7},{7,6},{8,9},{9,8},{10,11... | collective-permute-start | bytes 393224 | tf_op jit(solution)/shard_map/ppermute | solution.py:260
  23.2 1.4 %collective-permute-start.7 = (bf16[32,2048]{1,0:T(8,128)(2,1)S(1)}, bf16[32,2048]{1,0:T(8,128)(2,1)S(1)}, u32[]{:S(2)}, u32[]{:S(2)}) collective-permute-start(bf16[32,2048]{1,0:T(8,128)(2,1)S(1)} %get-tuple-element.18), channel_id=1, source_target_pairs={{0,1},{1,0},{2,3},{3,2},{4,5},{5,4},{6,7},{7,6},{8,9},{9,8},{10,11... | collective-permute-start | bytes 393224 | tf_op jit(solution)/shard_map/ppermute | solution.py:260
  24.7 3.9 %collective-permute-start.8 = (bf16[16,2048]{1,0:T(8,128)(2,1)S(1)}, bf16[16,2048]{1,0:T(8,128)(2,1)S(1)}, u32[]{:S(2)}, u32[]{:S(2)}) collective-permute-start(bf16[16,2048]{1,0:T(8,128)(2,1)S(1)} %get-tuple-element.20), channel_id=1, source_target_pairs={{0,3},{1,2},{2,1},{3,0},{4,7},{5,6},{6,5},{7,4},{8,11},{9,10},{10,... | collective-permute-start | bytes 196616 | tf_op jit(solution)/shard_map/ppermute | solution.py:260
  28.7 4.2 %collective-permute-start.9 = (bf16[4,2048]{1,0:T(4,128)(2,1)S(1)}, bf16[4,2048]{1,0:T(4,128)(2,1)S(1)}, u32[]{:S(2)}, u32[]{:S(2)}) collective-permute-start(bf16[4,2048]{1,0:T(4,128)(2,1)S(1)} %get-tuple-element.22), channel_id=1, source_target_pairs={{0,4},{1,5},{2,6},{3,7},{4,0},{5,1},{6,2},{7,3},{8,12},{9,13},{10,... | collective-permute-start | bytes 49160 | tf_op jit(solution)/shard_map/ppermute | solution.py:260
  29.5 4.2 %collective-permute-start.10 = (bf16[4,2048]{1,0:T(4,128)(2,1)S(1)}, bf16[4,2048]{1,0:T(4,128)(2,1)S(1)}, u32[]{:S(2)}, u32[]{:S(2)}) collective-permute-start(bf16[4,2048]{1,0:T(4,128)(2,1)S(1)} %get-tuple-element.23), channel_id=1, source_target_pairs={{0,9},{1,8},{2,11},{3,10},{4,13},{5,12},{6,15},{7,14},{8,1},{9,0},... | collective-permute-start | bytes 49160 | tf_op jit(solution)/shard_map/ppermute | solution.py:260
  31.3 5.0 %collective-permute-start.11 = (bf16[4,2048]{1,0:T(4,128)(2,1)S(1)}, bf16[4,2048]{1,0:T(4,128)(2,1)S(1)}, u32[]{:S(2)}, u32[]{:S(2)}) collective-permute-start(bf16[4,2048]{1,0:T(4,128)(2,1)S(1)} %get-tuple-element.24), channel_id=1, source_target_pairs={{0,13},{1,12},{2,15},{3,14},{4,9},{5,8},{6,11},{7,10},{8,5},{9,4},... | collective-permute-start | bytes 49160 | tf_op jit(solution)/shard_map/ppermute | solution.py:260
